TPU v7x, 256 devices: a whole 4x4x8 slice. The times are simulated.
256 devices in a mesh: pb: 16 (over y, x_hi, core), ga: 16 (over z, x_lo).
Axes of the slice: x: 4 (x_hi: 2, x_lo: 2; x = x_hi * 2 + x_lo), y: 4, z: 8, core: 2. Of those that a mesh axis runs over, the one named last changes fastest.
Arguments:
- elements: bfloat16 [16, 64, 112, 2048], P('pb', None, None, 'ga'), may hold values from -0.75 to 0.75
- screened: bfloat16 [16, 2048, 2048], P('pb', 'ga'), may hold values from -0.125 to 0.125
- counts: int32 [16], P('pb'), may hold values from 1536 to 2048
- k_minus_q: int32 [16], P('pb'), may hold values from 0 to 575
- occupation: float32 [576, 64], replicated, may hold values from 0.25 to 1
Outputs:
- sigma: float32 [112, 112], P('ga')
Inputs may be any that keep to these rules, and one draw needn't show every extreme that they name: k_minus_q[q] is a row of occupation.
All inputs are finite; a program needn't handle non-finite values.
Results may differ from a plain program's by a relative error of at most 0.0029.
Values may be sent and summed in bfloat16 or wider, within the bound.
No kernel may reach another device: no remote copies, remote signals or barrier semaphores. Data moves between devices by JAX's collectives and lax.ppermute only.
A program may use at most 128 MiB of HBM per device.

v0:
```python
import jax
import jax.numpy as jnp
from jax import lax
from jax.sharding import PartitionSpec as P

NB = 32


def on_device(elements, screened, counts, k_minus_q, occupation):
    q_count, n_band, n_state, g_slab = elements.shape
    groups = lax.axis_size("ga")
    my_index = lax.axis_index("ga")
    g_total = g_slab * groups
    n_cycles = g_total // (groups * NB)
    rows_true = my_index * g_slab + jnp.arange(g_slab, dtype=jnp.int32)
    inside = (rows_true[None, :] < counts[:, None]).astype(jnp.bfloat16)
    masked = elements * inside[:, None, None, :]
    k_index = jnp.arange(occupation.shape[0], dtype=jnp.int32)
    weights = jnp.sum(
        jnp.where(
            k_index[None, :, None] == k_minus_q[:, None, None], occupation[None], jnp.float32(0.0)
        ),
        axis=1,
    )
    partial_value = jnp.zeros((n_state, n_state), jnp.float32)
    columns = lax.all_to_all(screened, "ga", split_axis=2, concat_axis=1, tiled=True)
    columns = (
        columns.reshape(q_count, groups, n_cycles, NB, g_slab)
        .transpose(0, 2, 1, 3, 4)
        .reshape(q_count, g_total, g_slab)
    )

    def accumulate(running, segment, offset, screen_q=columns[0]):
        piece_rows = segment.shape[2]
        return jnp.dot(
            segment.reshape(n_band * n_state, piece_rows),
            screen_q,
            preferred_element_type=jnp.float32,
        )

    start_sum = jnp.zeros((n_band * n_state, g_slab), jnp.float32)
    product = accumulate(
        start_sum, lax.all_gather(masked[0], "ga", axis=2, tiled=True), jnp.int32(0)
    )
    product = product.astype(jnp.bfloat16).reshape(n_band, n_state, g_slab)
    pair_terms = jnp.einsum("vmg,vng->vmn", product, masked[0], preferred_element_type=jnp.float32)
    partial_value = partial_value - jnp.einsum(
        "v,vmn->mn", weights[0], pair_terms, precision=lax.Precision.HIGHEST
    )
    row_share = lax.psum_scatter(partial_value, "ga", scatter_dimension=0, tiled=True)
    result_rows = lax.psum(row_share, "pb")
    return result_rows


def solution(mesh):
    return jax.shard_map(
        on_device,
        mesh=mesh,
        in_specs=(P("pb", None, None, "ga"), P("pb", "ga", None), P("pb"), P("pb"), P()),
        out_specs=P("ga", None),
        check_vma=False,
    )
```

profile of v0, /device:TPU:1, one launch (start us, length us, event | category | flops | bytes accessed | tf_op | source)
XLA Modules:
  0.0 744.2 jit_solution(9691880198805703079)
XLA Ops:
  6.5 0.0 all-gather.3.cloned.1.call-start
  7.2 2.9 broadcast_multiply_fusion
  10.1 0.0 all-gather.3.cloned.1.call-update
  10.1 1.0 copy-done.1
  11.1 0.7 copy.10
  11.9 0.5 broadcast.22
  12.4 11.6 %reduce.2 = bf16[2048,128]{1,0:T(8,128)(2,1)S(1)} reduce(bf16[2048,1,128]{2,1,0:T(2,128)(2,1)S(1)} %bitcast.28, bf16[]{:T(256)} %broadcast.22), dimensions={1}, to_apply=%bitcast.20.reduce_sub_computation | reduce | bytes 1048578
  24.0 0.9 reshape.45
  24.9 10.1 %all-to-all-start = ((bf16[16,2,8192]{2,1,0:T(2,128)(2,1)}), bf16[16,2,8192]{2,1,0:T(2,128)(2,1)S(1)}, u32[]{:S(2)}, u32[]{:S(2)}) async-start(bf16[16,2,8192]{2,1,0:T(2,128)(2,1)} %reshape.45), calls=%async_computation | async-start | bytes 1048576 | tf_op jit(solution)/shard_map/all_to_all | solution.py:26
  35.6 0.0 copy-done.3
  35.6 0.6 dynamic-slice
  36.8 0.0 copy-done.2
  36.8 0.1 select_reduce_fusion
  36.9 20.0 %all-to-all-done = bf16[16,2,8192]{2,1,0:T(2,128)(2,1)S(1)} async-done(((bf16[16,2,8192]{2,1,0:T(2,128)(2,1)}), bf16[16,2,8192]{2,1,0:T(2,128)(2,1)S(1)}, u32[]{:S(2)}, u32[]{:S(2)}) %all-to-all-start) | async-done | bytes 524320 | tf_op jit(solution)/shard_map/all_to_all | solution.py:26
  56.9 0.5 reshape.46
  57.5 0.1 copy.15
  57.6 0.3 copy.11
  57.9 564.0 %all-gather.3.cloned.1.call-done = bf16[1,64,112,2048]{3,2,1,0:T(8,128)(2,1)} async-done(((bf16[1,64,112,128]{3,2,1,0:T(8,128)(2,1)}), bf16[1,64,112,2048]{3,2,1,0:T(8,128)(2,1)}) %all-gather.3.cloned.1.call-update) | async-done | bytes 29360144 | tf_op jit(solution)/shard_map/all_gather | solution.py:43
  621.9 13.7 %convolution_convert_fusion = bf16[7168,128]{1,0:T(8,128)(2,1)S(1)} fusion(bf16[7168,2048]{1,0:T(8,128)(2,1)} %bitcast.34, bf16[2048,128]{1,0:T(8,128)(2,1)S(1)} %bitcast.32), kind=kOutput, calls=%fused_computation | convolution fusion | flops 3759013888 | bytes 31719424 | tf_op jit(solution)/shard_map/dot_general | solution.py:35
  635.6 0.0 copy-done
  635.6 1.1 fusion.2
  636.7 2.8 fusion
  639.5 49.6 %all-reduce = f32[112,112]{1,0:T(8,128)S(1)} all-reduce(f32[112,112]{1,0:T(8,128)S(1)} %broadcast_subtract_fusion), channel_id=3, replica_groups=mesh['pb'=16,'ga'=16] {'ga'}, use_global_device_ids=true, to_apply=%region_1.2.clone | all-reduce | flops 12544 | bytes 100352
  689.1 48.3 %psum.7 = f32[7,112]{1,0:T(8,128)} all-reduce(f32[7,112]{1,0:T(8,128)S(1)} %constant_dynamic-slice_fusion), channel_id=1, replica_groups=mesh['pb'=16,'ga'=16] {'pb'}, use_global_device_ids=true, to_apply=%region_2.3 | all-reduce | flops 784 | bytes 6272 | tf_op jit(solution)/shard_map/psum | solution.py:51
  (9 shorter events, 0.1 us)
Async XLA Ops:
  6.5 615.4 %all-gather.3.cloned.1.call-start = ((), (), s32[]{:S(2)}) async-start(), calls=%async_computation.1 | async-start | bytes 31195136 | tf_op jit(solution)/shard_map/all_gather | solution.py:43
  10.1 1.0 copy-start.1
  12.4 23.2 %copy-start.3 = (u32[256]{0:T(256)S(1)}, u32[256]{0:T(256)}, u32[]{:S(2)}) copy-start(u32[256]{0:T(256)} %constant.15) | copy-start | bytes 3076
  12.4 24.4 %copy-start.2 = (f32[576,64]{0,1:T(8,128)S(1)}, f32[576,64]{0,1:T(8,128)}, u32[]{:S(2)}) copy-start(f32[576,64]{0,1:T(8,128)} %param.9) | copy-start | bytes 442372
  24.9 32.1 %all-to-all-start = ((bf16[16,2,8192]{2,1,0:T(2,128)(2,1)}), bf16[16,2,8192]{2,1,0:T(2,128)(2,1)S(1)}, u32[]{:S(2)}, u32[]{:S(2)}) async-start(bf16[16,2,8192]{2,1,0:T(2,128)(2,1)} %reshape.45), calls=%async_computation | async-start | bytes 1048576 | tf_op jit(solution)/shard_map/all_to_all | solution.py:26
  621.9 13.7 %copy-start = (bf16[1,64,112,128]{3,2,1,0:T(8,128)(2,1)S(1)}, bf16[1,64,112,128]{3,2,1,0:T(8,128)(2,1)}, u32[]{:S(2)}) copy-start(bf16[1,64,112,128]{3,2,1,0:T(8,128)(2,1)} %broadcast_multiply_fusion) | copy-start | bytes 5505028
Sparse Core Ops, SparseCore 0:
  10.2 611.6 all-gather.2
where the time goes:
time: 745 us; the launch traced here: 744 us
  waiting for transfers between devices  584 us (78%)
  blocking collectives  97.8 us (13%)
  matrix products  17.5 us (2%)
  between operations  15.4 us (2%)
  other arithmetic  14.6 us (2%)
  starting transfers between devices  10.1 us (1%)
    all_gather x1, waiting for transfers between devices, on_device(): lax.all_gather(masked[0], 'ga', axis=2, tiled=True)  564 us
    unnamed x1, blocking collectives  49.6 us
    psum x1, blocking collectives, on_device(): result_rows = lax.psum(row_share, 'pb')  48.3 us
    all_to_all x1, waiting for transfers between devices, on_device(): lax.all_to_all(screened, 'ga', split_axis=2, concat_axis=1, tiled=True)  20 us
  transfers between devices with their start and end apart: 2, of which 2 were waited for; matrix products, arithmetic and copies ran while one was open for 2% of the time, Pallas kernels for 0%

commit v1 on v0

v1 whole, which is shorter than its diff:
```python
import functools

import jax
import jax.numpy as jnp
from jax import lax
from jax.experimental import pallas as pl
from jax.experimental.pallas import tpu as pltpu
from jax.sharding import PartitionSpec as P

NB = 32
LANES = 128


def split_columns(scalars, stored, keep, send):
    me, count = scalars[0], scalars[1]
    x = lax.rem(me, 2)
    rows = stored.shape[0]
    row = lax.broadcasted_iota(jnp.int32, (rows, LANES), 0)
    lane = lax.broadcasted_iota(jnp.int32, (rows, LANES), 1)
    true_row = ((row // NB) * 16 + me) * NB + row % NB
    for s in range(keep.shape[1] // LANES):
        for out, parity in ((keep, x), (send, 1 - x)):
            first = pl.multiple_of((2 * s + parity) * LANES, LANES)
            inside = (true_row < count) & (lane + first < count)
            block = stored[:, pl.ds(first, LANES)].astype(jnp.float32)
            out[:, s * LANES : (s + 1) * LANES] = jnp.where(inside, block, 0.0).astype(out.dtype)


def contract(scalars, weights, own, other, w_keep, w_recv, sigma, w_sorted):
    x = lax.rem(scalars[0], 2)
    n_z, bands, states, _ = own.shape

    @pl.when(pl.program_id(0) == 0)
    def _():
        sigma[...] = jnp.zeros_like(sigma)
        for s in range(n_z):
            for slot in range(2):
                quarter = 2 * (s % 2) + (slot + x) % 2
                for u in range(2):
                    base = (2 * s + slot) * LANES + 2 * u * NB
                    w_sorted[pl.ds(pl.multiple_of(base + x * NB, NB), NB), :] = w_keep[2 * quarter + u, s // 2]
                    w_sorted[pl.ds(pl.multiple_of(base + (1 - x) * NB, NB), NB), :] = w_recv[2 * quarter + u, s // 2]

    lhs = jnp.concatenate(
        [part[s].reshape(bands * states, LANES) for s in range(n_z) for part in (own, other)], axis=1
    )
    product = jnp.dot(lhs, w_sorted[...], preferred_element_type=jnp.float32).astype(jnp.bfloat16)
    total = jnp.zeros((states, states), jnp.float32)
    for b in range(bands):
        right = jnp.concatenate([own[s, b] for s in range(n_z)], axis=1)
        pair = lax.dot_general(
            product[b * states : (b + 1) * states],
            right,
            (((1,), (1,)), ((), ())),
            preferred_element_type=jnp.float32,
        )
        total = total + weights[pl.program_id(0) * bands + b] * pair
    sigma[...] -= total


def on_device(elements, screened, counts, k_minus_q, occupation):
    _, n_band, n_state, g_slab = elements.shape
    groups = lax.axis_size("ga")
    n_z = groups // 2
    me = lax.axis_index("ga").astype(jnp.int32)
    z_groups = [[2 * z + x for z in range(n_z)] for x in range(2)]
    swap_x = [(i, i ^ 1) for i in range(groups)]
    scalars = jnp.stack([me, counts[0]])
    half = screened.shape[2] // 2

    keep, send = pl.pallas_call(
        split_columns,
        out_shape=[jax.ShapeDtypeStruct((g_slab, half), jnp.bfloat16)] * 2,
        in_specs=[pl.BlockSpec(memory_space=pltpu.SMEM), pl.BlockSpec(memory_space=pltpu.VMEM)],
        out_specs=[pl.BlockSpec(memory_space=pltpu.VMEM)] * 2,
    )(scalars, screened[0])
    recv = lax.ppermute(send, "ga", swap_x)
    w_keep = lax.all_gather(keep, "ga", axis_index_groups=z_groups)
    w_recv = lax.all_gather(recv, "ga", axis_index_groups=z_groups)

    own = lax.all_to_all(elements[0], "ga", 0, 0, axis_index_groups=z_groups, tiled=True)
    other = lax.ppermute(own, "ga", swap_x)
    bands = n_band // n_z
    own = own.reshape(n_z, bands, n_state, g_slab)
    other = other.reshape(n_z, bands, n_state, g_slab)
    w_keep = w_keep.reshape(n_z, g_slab // NB, NB, half)
    w_recv = w_recv.reshape(n_z, g_slab // NB, NB, half)
    weights = lax.dynamic_slice(occupation, (k_minus_q[0], (me // 2) * bands), (1, bands))[0]

    step = 2
    a_spec = pl.BlockSpec((n_z, step, n_state, g_slab), lambda i: (0, i, 0, 0))
    w_spec = pl.BlockSpec((n_z, g_slab // NB, NB, half), lambda i: (0, 0, 0, 0), pipeline_mode=pl.Buffered(1))
    partial_sum = pl.pallas_call(
        contract,
        grid=(bands // step,),
        out_shape=jax.ShapeDtypeStruct((n_state, n_state), jnp.float32),
        in_specs=[
            pl.BlockSpec(memory_space=pltpu.SMEM),
            pl.BlockSpec(memory_space=pltpu.SMEM),
            a_spec,
            a_spec,
            w_spec,
            w_spec,
        ],
        out_specs=pl.BlockSpec((n_state, n_state), lambda i: (0, 0)),
        scratch_shapes=[pltpu.VMEM((2 * half, half), jnp.bfloat16)],
        compiler_params=pltpu.CompilerParams(vmem_limit_bytes=48 * 1024 * 1024),
    )(scalars, weights, own, other, w_keep, w_recv)

    rows = n_state // groups
    shares = lax.all_to_all(partial_sum.reshape(groups, rows, n_state), "ga", 0, 0, tiled=True)
    share = jnp.sum(shares, axis=0)
    copies = jnp.broadcast_to(share[None], (lax.axis_size("pb"), rows, n_state))
    return jnp.sum(lax.all_to_all(copies, "pb", 0, 0, tiled=True), axis=0)


def solution(mesh):
    return jax.shard_map(
        on_device,
        mesh=mesh,
        in_specs=(P("pb", None, None, "ga"), P("pb", "ga", None), P("pb"), P("pb"), P()),
        out_specs=P("ga", None),
        check_vma=False,
    )
```

time: 745 us -> 171 us (0.23)
  waiting for transfers between devices: 584 us -> 99.4 us
  blocking collectives: 97.8 us -> 32 us
  matrix products: 17.5 us -> 0 us
  other arithmetic: 14.6 us -> 1.3 us
  Pallas kernels: 0 us -> 9.37 us
    all_gather x1 -> x2, waiting for transfers between devices: 564 us -> 39.4 us  [the longest x1 39.4 us: on_device(): w_recv = lax.all_gather(recv, 'ga', axis_index_groups=z_groups)]
    unnamed x1 -> x0, blocking collectives: 49.6 us -> none
    psum x1 -> x0, blocking collectives: 48.3 us -> none  [on_device(): result_rows = lax.psum(row_share, 'pb')]
    all_to_all x1, waiting for transfers between devices: 20 us -> 54.2 us  [on_device(): lax.all_to_all(elements[0], 'ga', 0, 0, axis_index_groups=z_groups, tiled...]
    all_to_all x0 -> x2, blocking collectives: none -> 32 us  [the longest x1 19.3 us: on_device(): return jnp.sum(lax.all_to_all(copies, 'pb', 0, 0, tiled=True), axis=0)]
    dot_general x3 -> x0, matrix products: 17.5 us -> none  [the longest x1 13.7 us: accumulate(): jnp.dot(segment.reshape(n_band * n_state, piece_rows), screen_q, preferre...]
    unnamed x1 -> x0, other arithmetic: 11.6 us -> none
    pallas_call x0 -> x2, Pallas kernels: none -> 9.37 us  [the longest x1 7.34 us: on_device(): pl.pallas_call(contract, grid=(bands // step,), out_shape=jax.ShapeDtypeS...]
  transfers between devices with their start and end apart: 2 -> 5, of which waited for: 2 -> 3; matrix products, arithmetic and copies ran while one was open for 2% -> 0% of each run, Pallas kernels for 0% -> 0%
where the time goes in v1:
time: 171 us
  waiting for transfers between devices  99.4 us (58%)
  blocking collectives  32 us (19%)
  between operations  14.8 us (9%)
  starting transfers between devices  11.5 us (7%)
  Pallas kernels  9.37 us (5%)
  local copies, waits for them, and re-layouts  2.5 us (1%)
    all_to_all x1, waiting for transfers between devices, on_device(): lax.all_to_all(elements[0], 'ga', 0, 0, axis_index_groups=z_groups, tiled...  54.2 us
    all_gather x1, waiting for transfers between devices, on_device(): w_recv = lax.all_gather(recv, 'ga', axis_index_groups=z_groups)  39.4 us
    all_to_all x1, blocking collectives, on_device(): return jnp.sum(lax.all_to_all(copies, 'pb', 0, 0, tiled=True), axis=0)  19.3 us
    all_to_all x1, blocking collectives, on_device(): lax.all_to_all(partial_sum.reshape(groups, rows, n_state), 'ga', 0, 0, ti...  12.7 us
    all_to_all x1, starting transfers between devices, on_device(): lax.all_to_all(elements[0], 'ga', 0, 0, axis_index_groups=z_groups, tiled...  9.16 us
    pallas_call x1, Pallas kernels, on_device(): pl.pallas_call(contract, grid=(bands // step,), out_shape=jax.ShapeDtypeS...  7.34 us
    ppermute x1, waiting for transfers between devices, on_device(): recv = lax.ppermute(send, 'ga', swap_x)  5.65 us
  transfers between devices with their start and end apart: 5, of which 3 were waited for; matrix products, arithmetic and copies ran while one was open for 0% of the time, Pallas kernels for 0%

profile of v1, /device:TPU:1, one launch (start us, length us, event | category | flops | bytes accessed | tf_op | source)
XLA Modules:
  0.0 170.8 jit_solution(17550952057627708302)
XLA Ops:
  6.5 0.0 copy-start
  6.5 0.0 all-gather.5.cloned.1.call-start
  7.2 0.7 pad_add_fusion.scalars
  7.9 2.0 %shard_map.55 = (bf16[128,1024]{1,0:T(8,128)(2,1)}, bf16[128,1024]{1,0:T(8,128)(2,1)}) custom-call(s32[2]{0:T(128)} %pad_add_fusion.scalars, bf16[128,2048]{1,0:T(8,128)(2,1)} %bitcast.15), custom_call_target="tpu_custom_call" | custom-call | tf_op jit(solution)/shard_map/pallas_call | solution.py:71
  9.9 0.0 all-gather.5.cloned.1.call-update
  9.9 0.0 copy-start.4
  10.0 0.0 copy-start.2
  10.0 9.2 %all-to-all-start = ((bf16[64,112,128]{2,1,0:T(8,128)(2,1)}), bf16[64,112,128]{2,1,0:T(8,128)(2,1)S(1)}, u32[]{:S(2)}, u32[]{:S(2)}) async-start(bf16[64,112,128]{2,1,0:T(8,128)(2,1)} %bitcast.14), calls=%async_computation | async-start | bytes 3670016 | tf_op jit(solution)/shard_map/all_to_all | solution.py:81
  19.1 0.0 all-gather.7.cloned.1.call-start
  19.2 1.3 collective-permute-start.1
  20.5 5.6 %collective-permute-done.1 = bf16[128,1024]{1,0:T(8,128)(2,1)S(1)} collective-permute-done((bf16[128,1024]{1,0:T(8,128)(2,1)S(1)}, bf16[128,1024]{1,0:T(8,128)(2,1)S(1)}, u32[]{:S(2)}, u32[]{:S(2)}) %collective-permute-start.1) | collective-permute-done | bytes 262176 | tf_op jit(solution)/shard_map/ppermute | solution.py:77
  26.1 0.7 copy-done.3
  26.8 0.0 all-gather.7.cloned.1.call-update
  26.8 54.2 %all-to-all-done = bf16[64,112,128]{2,1,0:T(8,128)(2,1)S(1)} async-done(((bf16[64,112,128]{2,1,0:T(8,128)(2,1)}), bf16[64,112,128]{2,1,0:T(8,128)(2,1)S(1)}, u32[]{:S(2)}, u32[]{:S(2)}) %all-to-all-start) | async-done | bytes 1835040 | tf_op jit(solution)/shard_map/all_to_all | solution.py:81
  81.1 1.0 collective-permute-start
  82.7 0.2 dynamic-slice_reduce_fusion.weights
  82.9 0.0 all-gather.5.cloned.1.call-done
  82.9 39.4 %all-gather.7.cloned.1.call-done = bf16[1024,1024]{1,0:T(8,128)(2,1)} async-done(((bf16[128,1024]{1,0:T(8,128)(2,1)}), bf16[1024,1024]{1,0:T(8,128)(2,1)}) %all-gather.7.cloned.1.call-update) | async-done | bytes 2097168 | tf_op jit(solution)/shard_map/all_gather | solution.py:79
  122.4 0.0 collective-permute-done
  122.4 1.6 copy-done.1
  124.0 7.3 %shard_map.56 = f32[112,112]{1,0:T(8,128)S(1)} custom-call(s32[2]{0:T(128)S(1)} %copy-done.2, f32[8]{0:T(128)S(1)} %dynamic-slice_reduce_fusion.weights, bf16[8,8,112,128]{3,2,1,0:T(8,128)(2,1)S(1)} %bitcast.11, bf16[8,8,112,128]{3,2,1,0:T(8,128)(2,1)} %bitcast.4.other, bf16[8,4,32,1024]{3,2,1,0:T(8,128)(2,1)S(1)} %bitcast.12, bf16[8,4,32,1024]{3,2,1,0:T(8,128)(2,1)} %bitcast.13), custom_call_target="tpu_custom_call" | custom-call | tf_op jit(solution)/shard_map/pallas_call | solution.py:93
  131.3 12.7 %all_to_all.15 = f32[16,7,112]{2,1,0:T(8,128)S(1)} all-to-all(f32[16,7,112]{2,1,0:T(8,128)S(1)} %reshape.20), channel_id=1, replica_groups=mesh['pb'=16,'ga'=16] {'ga'}, dimensions={0} | all-to-all | bytes 100352 | tf_op jit(solution)/shard_map/all_to_all | solution.py:111
  144.1 19.3 %all_to_all.16 = f32[16,7,112]{2,1,0:T(8,128)S(1)} all-to-all(f32[16,7,112]{2,1,0:T(8,128)S(1)} %broadcast_in_dim.2), channel_id=1, replica_groups=mesh['pb'=16,'ga'=16] {'pb'}, dimensions={0} | all-to-all | bytes 100352 | tf_op jit(solution)/shard_map/all_to_all | solution.py:114
  163.4 0.6 reduce_sum.19
  (8 shorter events, 0.0 us)
Async XLA Ops:
  6.5 76.2 %copy-start = (f32[576,64]{0,1:T(8,128)S(1)}, f32[576,64]{0,1:T(8,128)}, u32[]{:S(2)}) copy-start(f32[576,64]{0,1:T(8,128)} %param.9) | copy-start | bytes 442372
  6.5 76.4 %all-gather.5.cloned.1.call-start = ((), (), s32[]{:S(2)}) async-start(), calls=%async_computation.3 | async-start | bytes 2359296 | tf_op jit(solution)/shard_map/all_gather | solution.py:78
  9.9 9.2 %copy-start.4 = (bf16[128,1024]{1,0:T(8,128)(2,1)S(1)}, bf16[128,1024]{1,0:T(8,128)(2,1)}, u32[]{:S(2)}) copy-start(bf16[128,1024]{1,0:T(8,128)(2,1)} %get-tuple-element.8) | copy-start | bytes 786436
  10.0 112.4 %copy-start.2 = (s32[2]{0:T(128)S(1)}, s32[2]{0:T(128)}, u32[]{:S(2)}) copy-start(s32[2]{0:T(128)} %pad_add_fusion.scalars) | copy-start | bytes 28
  10.0 71.1 %all-to-all-start = ((bf16[64,112,128]{2,1,0:T(8,128)(2,1)}), bf16[64,112,128]{2,1,0:T(8,128)(2,1)S(1)}, u32[]{:S(2)}, u32[]{:S(2)}) async-start(bf16[64,112,128]{2,1,0:T(8,128)(2,1)} %bitcast.14), calls=%async_computation | async-start | bytes 3670016 | tf_op jit(solution)/shard_map/all_to_all | solution.py:81
  19.1 103.2 %all-gather.7.cloned.1.call-start = ((), (), s32[]{:S(2)}) async-start(), calls=%async_computation.4 | async-start | bytes 2359296 | tf_op jit(solution)/shard_map/all_gather | solution.py:79
  19.2 6.9 %collective-permute-start.1 = (bf16[128,1024]{1,0:T(8,128)(2,1)S(1)}, bf16[128,1024]{1,0:T(8,128)(2,1)S(1)}, u32[]{:S(2)}, u32[]{:S(2)}) collective-permute-start(bf16[128,1024]{1,0:T(8,128)(2,1)S(1)} %copy-done.4), channel_id=1, source_target_pairs={{0,1},{1,0},{2,3},{3,2},{4,5},{5,4},{6,7},{7,6},{8,9},{9,8},{10,11... | collective-permute-start | bytes 786440 | tf_op jit(solution)/shard_map/ppermute | solution.py:77
  26.1 0.7 copy-start.3
  81.1 41.3 %collective-permute-start = (bf16[64,112,128]{2,1,0:T(8,128)(2,1)S(1)}, bf16[64,112,128]{2,1,0:T(8,128)(2,1)}, u32[]{:S(2)}, u32[]{:S(2)}) collective-permute-start(bf16[64,112,128]{2,1,0:T(8,128)(2,1)S(1)} %all-to-all-done), channel_id=1, source_target_pairs={{0,1},{1,0},{2,3},{3,2},{4,5},{5,4},{6,7},{7,6},{8,9},{9,8},{10,11... | collective-permute-start | bytes 5505032 | tf_op jit(solution)/shard_map/ppermute | solution.py:82
  122.4 1.6 copy-start.1
Sparse Core Ops, SparseCore 0:
  10.1 72.1 all-gather.4
  84.1 38.2 all-gather.6

commit v2 on v0

v2 whole, which is shorter than its diff:
```python
import functools

import jax
import jax.numpy as jnp
from jax import lax
from jax.experimental import pallas as pl
from jax.experimental.pallas import tpu as pltpu
from jax.sharding import PartitionSpec as P

NB = 32
LANES = 128
SPACE = pltpu.VMEM


def prepare(bands, counts, k_minus_q, occupation, stored, keep, send, weights):
    me, count = lax.axis_index("ga"), counts[0]
    x = lax.rem(me, 2)
    rows = stored.shape[1]
    row = lax.broadcasted_iota(jnp.int32, (rows, LANES), 0)
    lane = lax.broadcasted_iota(jnp.int32, (rows, LANES), 1)
    true_row = ((row // NB) * 16 + me) * NB + row % NB
    for s in range(keep.shape[1] // LANES):
        for out, parity in ((keep, x), (send, 1 - x)):
            first = pl.multiple_of((2 * s + parity) * LANES, LANES)
            inside = (true_row < count) & (lane + first < count)
            block = stored[0, :, pl.ds(first, LANES)].astype(jnp.float32)
            out[:, s * LANES : (s + 1) * LANES] = jnp.where(inside, block, 0.0).astype(out.dtype)
    row_k = occupation[pl.ds(k_minus_q[0], 1), :]
    band = lax.broadcasted_iota(jnp.int32, row_k.shape, 1)
    for b in range(bands):
        weights[b] = jnp.sum(jnp.where(band == (me // 2) * bands + b, row_k, 0.0))


def contract(n_z, weights, *refs):
    own, other = refs[:n_z], refs[n_z : 2 * n_z]
    rings = refs[2 * n_z : 3 * n_z], refs[3 * n_z : 4 * n_z]
    sigma, a_sorted, w_sorted = refs[4 * n_z :]
    me = lax.axis_index("ga")
    x, z = lax.rem(me, 2), me // 2
    bands, states, rows = own[0].shape

    for k in range(n_z):
        source = lax.rem(z + n_z - k, n_z)
        a_sorted[2 * source + x] = own[k][...]
        a_sorted[2 * source + 1 - x] = other[k][...]
        for ring, x_of in zip(rings, (x, 1 - x)):
            for c in range(rows // NB):
                to = (4 * c + source // 2) * LANES + (2 * lax.rem(source, 2) + x_of) * NB
                w_sorted[pl.ds(pl.multiple_of(to, NB), NB), :] = ring[k][c * NB : (c + 1) * NB, :]

    step = 2

    def some_bands(at, total):
        b = at * step
        lhs = jnp.concatenate(
            [a_sorted[i, pl.ds(b, step)].reshape(step * states, LANES) for i in range(2 * n_z)], axis=1
        )
        product = jnp.dot(lhs, w_sorted[...], preferred_element_type=jnp.float32).astype(jnp.bfloat16)
        for j in range(step):
            right = jnp.concatenate([a_sorted[2 * s + x, b + j] for s in range(n_z)], axis=1)
            pair = lax.dot_general(
                product[j * states : (j + 1) * states],
                right,
                (((1,), (1,)), ((), ())),
                preferred_element_type=jnp.float32,
            )
            total = total - weights[b + j] * pair
        return total

    sigma[...] = lax.fori_loop(0, bands // step, some_bands, jnp.zeros((states, states), jnp.float32))


def on_device(elements, screened, counts, k_minus_q, occupation):
    _, n_band, n_state, g_slab = elements.shape
    groups = lax.axis_size("ga")
    n_z = groups // 2
    z = lax.axis_index("ga") // 2
    bands = n_band // n_z
    half_columns = screened.shape[2] // 2

    def over_x(value):
        return lax.ppermute(value, "ga", [(i, i ^ 1) for i in range(groups)])

    def over_z(value, k):
        return lax.ppermute(value, "ga", [(i, (i + 2 * k) % groups) for i in range(groups)])

    keep, send, weights = pl.pallas_call(
        functools.partial(prepare, bands),
        out_shape=[jax.ShapeDtypeStruct((g_slab, half_columns), jnp.bfloat16)] * 2
        + [jax.ShapeDtypeStruct((bands,), jnp.float32)],
        in_specs=[pl.BlockSpec(memory_space=pltpu.SMEM)] * 2 + [pl.BlockSpec(memory_space=pltpu.VMEM)] * 2,
        out_specs=[pl.BlockSpec(memory_space=pltpu.VMEM)] * 2 + [pl.BlockSpec(memory_space=pltpu.SMEM)],
    )(counts, k_minus_q, occupation, screened)

    slabs = elements[0].reshape(n_z, bands, n_state, g_slab)
    own, other = [None] * n_z, [None] * n_z
    for k in range(n_z):
        own[k] = lax.dynamic_index_in_dim(slabs, (z + k) % n_z, 0, keepdims=False)
    for k in range(1, n_z):
        own[k] = over_z(own[k], k)
    recv = over_x(send)
    tie = lax.optimization_barrier
    ring_k, ring_r = [keep] + [None] * (n_z - 1), [recv] + [None] * (n_z - 1)
    ring_k[0], own[1], own[7] = tie((ring_k[0], own[1], own[7]))
    ring_k[1], ring_k[7] = over_z(ring_k[0], 1), over_z(ring_k[0], -1)
    ring_r[1], ring_r[7] = over_z(ring_r[0], 1), over_z(ring_r[0], -1)
    ring_k[1], ring_k[7], own[2], own[6] = tie((ring_k[1], ring_k[7], own[2], own[6]))
    ring_k[2], ring_k[6] = over_z(ring_k[1], 1), over_z(ring_k[7], -1)
    ring_r[2], ring_r[6] = over_z(ring_r[1], 1), over_z(ring_r[7], -1)
    ring_k[2], ring_k[6], own[3], own[5] = tie((ring_k[2], ring_k[6], own[3], own[5]))
    ring_k[3], ring_k[5] = over_z(ring_k[2], 1), over_z(ring_k[6], -1)
    ring_r[3], ring_r[5] = over_z(ring_r[2], 1), over_z(ring_r[6], -1)
    ring_k[3], own[4] = tie((ring_k[3], own[4]))
    ring_k[4], ring_r[4] = over_z(ring_k[3], 1), over_z(ring_r[5], -1)
    for k in range(n_z):
        other[k] = over_x(own[k])

    operands = [pltpu.with_memory_space_constraint(v, SPACE) for v in own + other + ring_k + ring_r]
    partial_sum = pl.pallas_call(
        functools.partial(contract, n_z),
        out_shape=jax.ShapeDtypeStruct((n_state, n_state), jnp.float32),
        in_specs=[pl.BlockSpec(memory_space=pltpu.SMEM)] + [pl.BlockSpec(memory_space=pltpu.VMEM)] * (4 * n_z),
        out_specs=pl.BlockSpec(memory_space=pltpu.VMEM),
        scratch_shapes=[
            pltpu.VMEM((groups, bands, n_state, g_slab), jnp.bfloat16),
            pltpu.VMEM((2 * half_columns, half_columns), jnp.bfloat16),
        ],
        compiler_params=pltpu.CompilerParams(vmem_limit_bytes=24 * 1024 * 1024),
    )(weights, *operands)

    rows = n_state // groups
    shares = lax.all_to_all(partial_sum.reshape(groups, rows, n_state), "ga", 0, 0, tiled=True)
    share = jnp.sum(shares, axis=0)
    copies = jnp.broadcast_to(share[None], (lax.axis_size("pb"), rows, n_state))
    return jnp.sum(lax.all_to_all(copies, "pb", 0, 0, tiled=True), axis=0)


def solution(mesh):
    return jax.shard_map(
        on_device,
        mesh=mesh,
        in_specs=(P("pb", None, None, "ga"), P("pb", "ga", None), P("pb"), P("pb"), P()),
        out_specs=P("ga", None),
        check_vma=False,
    )
```

time: 745 us -> 141 us (0.19)
  waiting for transfers between devices: 584 us -> 43.8 us
  blocking collectives: 97.8 us -> 34.2 us
  starting transfers between devices: 10.1 us -> 47.9 us
  matrix products: 17.5 us -> 0 us
  between operations: 15.4 us -> 1.38 us
  other arithmetic: 14.6 us -> 0.63 us
  Pallas kernels: 0 us -> 8.73 us
    all_gather x1 -> x0, waiting for transfers between devices: 564 us -> none  [on_device(): lax.all_gather(masked[0], 'ga', axis=2, tiled=True)]
    unnamed x1 -> x0, blocking collectives: 49.6 us -> none
    psum x1 -> x0, blocking collectives: 48.3 us -> none  [on_device(): result_rows = lax.psum(row_share, 'pb')]
    ppermute x0 -> x30, starting transfers between devices: none -> 47.9 us  [the longest x21 41.6 us: over_z(): lax.ppermute(value, 'ga', [(i, (i + 2 * k) % groups) for i in range(group...]
    ppermute x0 -> x30, waiting for transfers between devices: none -> 43.8 us  [the longest x21 29.6 us: over_z(): lax.ppermute(value, 'ga', [(i, (i + 2 * k) % groups) for i in range(group...]
    all_to_all x0 -> x2, blocking collectives: none -> 34.2 us  [the longest x1 18 us: on_device(): return jnp.sum(lax.all_to_all(copies, 'pb', 0, 0, tiled=True), axis=0)]
    all_to_all x1 -> x0, waiting for transfers between devices: 20 us -> none  [on_device(): lax.all_to_all(screened, 'ga', split_axis=2, concat_axis=1, tiled=True)]
    dot_general x3 -> x0, matrix products: 17.5 us -> none  [the longest x1 13.7 us: accumulate(): jnp.dot(segment.reshape(n_band * n_state, piece_rows), screen_q, preferre...]
  transfers between devices with their start and end apart: 2 -> 30, of which waited for: 2 -> 11; matrix products, arithmetic and copies ran while one was open for 2% -> 1% of each run, Pallas kernels for 0% -> 2%
where the time goes in v2:
time: 141 us
  starting transfers between devices  47.9 us (34%)
  waiting for transfers between devices  43.8 us (31%)
  blocking collectives  34.2 us (24%)
  Pallas kernels  8.73 us (6%)
  local copies, waits for them, and re-layouts  4.21 us (3%)
    ppermute x21, starting transfers between devices, over_z(): lax.ppermute(value, 'ga', [(i, (i + 2 * k) % groups) for i in range(group...  41.6 us
    ppermute x21, waiting for transfers between devices, over_z(): lax.ppermute(value, 'ga', [(i, (i + 2 * k) % groups) for i in range(group...  29.6 us
    all_to_all x1, blocking collectives, on_device(): return jnp.sum(lax.all_to_all(copies, 'pb', 0, 0, tiled=True), axis=0)  18 us
    all_to_all x1, blocking collectives, on_device(): lax.all_to_all(partial_sum.reshape(groups, rows, n_state), 'ga', 0, 0, ti...  16.3 us
    ppermute x9, waiting for transfers between devices, over_x(): return lax.ppermute(value, 'ga', [(i, i ^ 1) for i in range(groups)])  14.3 us
    pallas_call x1, Pallas kernels, on_device(): pl.pallas_call(functools.partial(contract, n_z), out_shape=jax.ShapeDtype...  6.58 us
    ppermute x9, starting transfers between devices, over_x(): return lax.ppermute(value, 'ga', [(i, i ^ 1) for i in range(groups)])  6.22 us
  transfers between devices with their start and end apart: 30, of which 11 were waited for; matrix products, arithmetic and copies ran while one was open for 1% of the time, Pallas kernels for 2%

profile of v2, /device:TPU:1, one launch (start us, length us, event | category | flops | bytes accessed | tf_op | source)
XLA Modules:
  0.0 140.9 jit_solution(1407202576383220388)
XLA Ops:
  1.7 6.5 %collective-permute-start.1 = (bf16[8,112,128]{2,1,0:T(8,128)(2,1)S(1)}, bf16[8,112,128]{2,1,0:T(8,128)(2,1)S(1)}, u32[]{:S(2)}, u32[]{:S(2)}) collective-permute-start(bf16[8,112,128]{2,1,0:T(8,128)(2,1)S(1)} %get-tuple-element.42), channel_id=1, source_target_pairs={{0,14},{1,15},{2,0},{3,1},{4,2},{5,3},{6,4},{7,5},{8,6},{9,7},{10,... | collective-permute-start | bytes 688136 | tf_op jit(solution)/shard_map/ppermute | solution.py:85
  10.4 2.1 %shard_map.55 = (bf16[128,1024]{1,0:T(8,128)(2,1)}, bf16[128,1024]{1,0:T(8,128)(2,1)}, f32[8]{0:T(128)}) custom-call(s32[1]{0:T(128)S(6)} %copy.12.counts, s32[1]{0:T(128)S(6)} %copy.13.k_minus_q, f32[576,64]{1,0:T(8,128)} %copy.9.occupation, bf16[1,128,2048]{2,1,0:T(8,128)(2,1)} %stored.1), custom_call_target="tpu_custom_call" | custom-call | tf_op jit(solution)/shard_map/pallas_call | solution.py:87
  13.8 1.9 %collective-permute-start.5 = (bf16[8,112,128]{2,1,0:T(8,128)(2,1)S(1)}, bf16[8,112,128]{2,1,0:T(8,128)(2,1)S(1)}, u32[]{:S(2)}, u32[]{:S(2)}) collective-permute-start(bf16[8,112,128]{2,1,0:T(8,128)(2,1)S(1)} %get-tuple-element.40), channel_id=1, source_target_pairs={{0,12},{1,13},{2,14},{3,15},{4,0},{5,1},{6,2},{7,3},{8,4},{9,5},{1... | collective-permute-start | bytes 688136 | tf_op jit(solution)/shard_map/ppermute | solution.py:85
  16.2 3.9 %collective-permute-start.3 = (bf16[128,1024]{1,0:T(8,128)(2,1)}, bf16[128,1024]{1,0:T(8,128)(2,1)S(1)}, u32[]{:S(2)}, u32[]{:S(2)}) collective-permute-start(bf16[128,1024]{1,0:T(8,128)(2,1)} %get-tuple-element.24.refs_16_), channel_id=1, source_target_pairs={{0,14},{1,15},{2,0},{3,1},{4,2},{5,3},{6,4},{7,5},{8,6},{9,7},{10,... | collective-permute-start | bytes 786440 | tf_op jit(solution)/shard_map/ppermute | solution.py:85
  20.1 2.7 %collective-permute-start.26 = (bf16[128,1024]{1,0:T(8,128)(2,1)S(1)}, bf16[128,1024]{1,0:T(8,128)(2,1)S(1)}, u32[]{:S(2)}, u32[]{:S(2)}) collective-permute-start(bf16[128,1024]{1,0:T(8,128)(2,1)S(1)} %collective-permute-done.22.refs_24_), channel_id=1, source_target_pairs={{0,14},{1,15},{2,0},{3,1},{4,2},{5,3},{6,4},{7,5},{8,6},{9,7},{10,... | collective-permute-start | bytes 786440 | tf_op jit(solution)/shard_map/ppermute | solution.py:85
  23.6 3.0 %collective-permute-start.9 = (bf16[8,112,128]{2,1,0:T(8,128)(2,1)S(1)}, bf16[8,112,128]{2,1,0:T(8,128)(2,1)S(1)}, u32[]{:S(2)}, u32[]{:S(2)}) collective-permute-start(bf16[8,112,128]{2,1,0:T(8,128)(2,1)S(1)} %get-tuple-element.38), channel_id=1, source_target_pairs={{0,10},{1,11},{2,12},{3,13},{4,14},{5,15},{6,0},{7,1},{8,2},{9,3},... | collective-permute-start | bytes 688136 | tf_op jit(solution)/shard_map/ppermute | solution.py:85
  26.7 3.8 %collective-permute-start.8 = (bf16[8,112,128]{2,1,0:T(8,128)(2,1)S(1)}, bf16[8,112,128]{2,1,0:T(8,128)(2,1)S(1)}, u32[]{:S(2)}, u32[]{:S(2)}) collective-permute-start(bf16[8,112,128]{2,1,0:T(8,128)(2,1)S(1)} %get-tuple-element.39), channel_id=1, source_target_pairs={{0,6},{1,7},{2,8},{3,9},{4,10},{5,11},{6,12},{7,13},{8,14},{9,15},... | collective-permute-start | bytes 688136 | tf_op jit(solution)/shard_map/ppermute | solution.py:85
  30.4 2.9 %collective-permute-done.3.refs_23_ = bf16[128,1024]{1,0:T(8,128)(2,1)S(1)} collective-permute-done((bf16[128,1024]{1,0:T(8,128)(2,1)}, bf16[128,1024]{1,0:T(8,128)(2,1)S(1)}, u32[]{:S(2)}, u32[]{:S(2)}) %collective-permute-start.3) | collective-permute-done | bytes 262176 | tf_op jit(solution)/shard_map/ppermute | solution.py:85
  33.4 3.1 %collective-permute-done.2.refs_17_ = bf16[128,1024]{1,0:T(8,128)(2,1)S(1)} collective-permute-done((bf16[128,1024]{1,0:T(8,128)(2,1)}, bf16[128,1024]{1,0:T(8,128)(2,1)S(1)}, u32[]{:S(2)}, u32[]{:S(2)}) %collective-permute-start.2) | collective-permute-done | bytes 262176 | tf_op jit(solution)/shard_map/ppermute | solution.py:85
  36.5 2.7 %collective-permute-start.7 = (bf16[128,1024]{1,0:T(8,128)(2,1)S(1)}, bf16[128,1024]{1,0:T(8,128)(2,1)S(1)}, u32[]{:S(2)}, u32[]{:S(2)}) collective-permute-start(bf16[128,1024]{1,0:T(8,128)(2,1)S(1)} %collective-permute-done.3.refs_23_), channel_id=1, source_target_pairs={{0,14},{1,15},{2,0},{3,1},{4,2},{5,3},{6,4},{7,5},{8,6},{9,7},{10,... | collective-permute-start | bytes 786440 | tf_op jit(solution)/shard_map/ppermute | solution.py:85
  39.2 8.6 %collective-permute-done.9.refs_5_ = bf16[8,112,128]{2,1,0:T(8,128)(2,1)S(1)} collective-permute-done((bf16[8,112,128]{2,1,0:T(8,128)(2,1)S(1)}, bf16[8,112,128]{2,1,0:T(8,128)(2,1)S(1)}, u32[]{:S(2)}, u32[]{:S(2)}) %collective-permute-start.9) | collective-permute-done | bytes 229408 | tf_op jit(solution)/shard_map/ppermute | solution.py:85
  47.8 2.8 %collective-permute-start.11 = (bf16[8,112,128]{2,1,0:T(8,128)(2,1)S(1)}, bf16[8,112,128]{2,1,0:T(8,128)(2,1)S(1)}, u32[]{:S(2)}, u32[]{:S(2)}) collective-permute-start(bf16[8,112,128]{2,1,0:T(8,128)(2,1)S(1)} %get-tuple-element.37), channel_id=1, source_target_pairs={{0,8},{1,9},{2,10},{3,11},{4,12},{5,13},{6,14},{7,15},{8,0},{9,1},... | collective-permute-start | bytes 688136 | tf_op jit(solution)/shard_map/ppermute | solution.py:85
  52.1 5.0 %collective-permute-done.6.refs_18_ = bf16[128,1024]{1,0:T(8,128)(2,1)S(1)} collective-permute-done((bf16[128,1024]{1,0:T(8,128)(2,1)S(1)}, bf16[128,1024]{1,0:T(8,128)(2,1)S(1)}, u32[]{:S(2)}, u32[]{:S(2)}) %collective-permute-start.6) | collective-permute-done | bytes 262176 | tf_op jit(solution)/shard_map/ppermute | solution.py:85
  57.1 6.1 %collective-permute-done.7.refs_22_ = bf16[128,1024]{1,0:T(8,128)(2,1)S(1)} collective-permute-done((bf16[128,1024]{1,0:T(8,128)(2,1)S(1)}, bf16[128,1024]{1,0:T(8,128)(2,1)S(1)}, u32[]{:S(2)}, u32[]{:S(2)}) %collective-permute-start.7) | collective-permute-done | bytes 262176 | tf_op jit(solution)/shard_map/ppermute | solution.py:85
  64.7 7.1 %collective-permute-start.10 = (bf16[128,1024]{1,0:T(8,128)(2,1)S(1)}, bf16[128,1024]{1,0:T(8,128)(2,1)S(1)}, u32[]{:S(2)}, u32[]{:S(2)}) collective-permute-start(bf16[128,1024]{1,0:T(8,128)(2,1)S(1)} %collective-permute-done.6.refs_18_), channel_id=1, source_target_pairs={{0,2},{1,3},{2,4},{3,5},{4,6},{5,7},{6,8},{7,9},{8,10},{9,11},{10,... | collective-permute-start | bytes 786440 | tf_op jit(solution)/shard_map/ppermute | solution.py:85
  71.9 2.9 %collective-permute-done.27.refs_30_ = bf16[128,1024]{1,0:T(8,128)(2,1)S(1)} collective-permute-done((bf16[128,1024]{1,0:T(8,128)(2,1)S(1)}, bf16[128,1024]{1,0:T(8,128)(2,1)S(1)}, u32[]{:S(2)}, u32[]{:S(2)}) %collective-permute-start.27) | collective-permute-done | bytes 262176 | tf_op jit(solution)/shard_map/ppermute | solution.py:85
  74.8 2.5 %collective-permute-start.28 = (bf16[128,1024]{1,0:T(8,128)(2,1)S(1)}, bf16[128,1024]{1,0:T(8,128)(2,1)S(1)}, u32[]{:S(2)}, u32[]{:S(2)}) collective-permute-start(bf16[128,1024]{1,0:T(8,128)(2,1)S(1)} %collective-permute-done.27.refs_30_), channel_id=1, source_target_pairs={{0,14},{1,15},{2,0},{3,1},{4,2},{5,3},{6,4},{7,5},{8,6},{9,7},{10,... | collective-permute-start | bytes 786440 | tf_op jit(solution)/shard_map/ppermute | solution.py:85
  79.0 3.8 %collective-permute-done.18.refs_14_ = bf16[8,112,128]{2,1,0:T(8,128)(2,1)S(1)} collective-permute-done((bf16[8,112,128]{2,1,0:T(8,128)(2,1)S(1)}, bf16[8,112,128]{2,1,0:T(8,128)(2,1)S(1)}, u32[]{:S(2)}, u32[]{:S(2)}) %collective-permute-start.18) | collective-permute-done | bytes 229408 | tf_op jit(solution)/shard_map/ppermute | solution.py:82
  84.4 3.3 %collective-permute-done.15.refs_11_ = bf16[8,112,128]{2,1,0:T(8,128)(2,1)S(1)} collective-permute-done((bf16[8,112,128]{2,1,0:T(8,128)(2,1)S(1)}, bf16[8,112,128]{2,1,0:T(8,128)(2,1)S(1)}, u32[]{:S(2)}, u32[]{:S(2)}) %collective-permute-start.15) | collective-permute-done | bytes 229408 | tf_op jit(solution)/shard_map/ppermute | solution.py:82
  90.4 2.2 %collective-permute-done.17.refs_13_ = bf16[8,112,128]{2,1,0:T(8,128)(2,1)S(1)} collective-permute-done((bf16[8,112,128]{2,1,0:T(8,128)(2,1)S(1)}, bf16[8,112,128]{2,1,0:T(8,128)(2,1)S(1)}, u32[]{:S(2)}, u32[]{:S(2)}) %collective-permute-start.17) | collective-permute-done | bytes 229408 | tf_op jit(solution)/shard_map/ppermute | solution.py:82
  92.9 4.9 %collective-permute-done.16.refs_12_ = bf16[8,112,128]{2,1,0:T(8,128)(2,1)S(1)} collective-permute-done((bf16[8,112,128]{2,1,0:T(8,128)(2,1)S(1)}, bf16[8,112,128]{2,1,0:T(8,128)(2,1)S(1)}, u32[]{:S(2)}, u32[]{:S(2)}) %collective-permute-start.16) | collective-permute-done | bytes 229408 | tf_op jit(solution)/shard_map/ppermute | solution.py:82
  99.4 6.6 %shard_map.56 = f32[112,112]{1,0:T(8,128)S(1)} custom-call(f32[8]{0:T(128)S(1)} %copy-done.1, bf16[8,112,128]{2,1,0:T(8,128)(2,1)S(1)} %get-tuple-element.44.refs_0_, bf16[8,112,128]{2,1,0:T(8,128)(2,1)S(1)} %collective-permute-done.refs_1_, bf16[8,112,128]{2,1,0:T(8,128)(2,1)S(1)} %collective-permute-done.4.refs_2_, ...), custom_call_target="tpu_custom_call" | custom-call | tf_op jit(solution)/shard_map/pallas_call | solution.py:119
  106.0 16.3 %all_to_all.10 = f32[16,7,112]{2,1,0:T(8,128)S(1)} all-to-all(f32[16,7,112]{2,1,0:T(8,128)S(1)} %reshape.4), channel_id=1, replica_groups=mesh['pb'=16,'ga'=16] {'ga'}, dimensions={0} | all-to-all | bytes 100352 | tf_op jit(solution)/shard_map/all_to_all | solution.py:132
  122.3 18.0 %all_to_all.11 = f32[16,7,112]{2,1,0:T(8,128)S(1)} all-to-all(f32[16,7,112]{2,1,0:T(8,128)S(1)} %broadcast_in_dim.2), channel_id=1, replica_groups=mesh['pb'=16,'ga'=16] {'pb'}, dimensions={0} | all-to-all | bytes 100352 | tf_op jit(solution)/shard_map/all_to_all | solution.py:135
  (52 shorter events, 16.8 us)
Async XLA Ops:
  1.7 14.5 %collective-permute-start.1 = (bf16[8,112,128]{2,1,0:T(8,128)(2,1)S(1)}, bf16[8,112,128]{2,1,0:T(8,128)(2,1)S(1)}, u32[]{:S(2)}, u32[]{:S(2)}) collective-permute-start(bf16[8,112,128]{2,1,0:T(8,128)(2,1)S(1)} %get-tuple-element.42), channel_id=1, source_target_pairs={{0,14},{1,15},{2,0},{3,1},{4,2},{5,3},{6,4},{7,5},{8,6},{9,7},{10,... | collective-permute-start | bytes 688136 | tf_op jit(solution)/shard_map/ppermute | solution.py:85
  15.7 10.9 %collective-permute-start.4 = (bf16[8,112,128]{2,1,0:T(8,128)(2,1)S(1)}, bf16[8,112,128]{2,1,0:T(8,128)(2,1)S(1)}, u32[]{:S(2)}, u32[]{:S(2)}) collective-permute-start(bf16[8,112,128]{2,1,0:T(8,128)(2,1)S(1)} %get-tuple-element.41), channel_id=1, source_target_pairs={{0,4},{1,5},{2,6},{3,7},{4,8},{5,9},{6,10},{7,11},{8,12},{9,13},{1... | collective-permute-start | bytes 688136 | tf_op jit(solution)/shard_map/ppermute | solution.py:85
  16.2 17.1 %collective-permute-start.3 = (bf16[128,1024]{1,0:T(8,128)(2,1)}, bf16[128,1024]{1,0:T(8,128)(2,1)S(1)}, u32[]{:S(2)}, u32[]{:S(2)}) collective-permute-start(bf16[128,1024]{1,0:T(8,128)(2,1)} %get-tuple-element.24.refs_16_), channel_id=1, source_target_pairs={{0,14},{1,15},{2,0},{3,1},{4,2},{5,3},{6,4},{7,5},{8,6},{9,7},{10,... | collective-permute-start | bytes 786440 | tf_op jit(solution)/shard_map/ppermute | solution.py:85
  20.1 16.4 %collective-permute-start.2 = (bf16[128,1024]{1,0:T(8,128)(2,1)}, bf16[128,1024]{1,0:T(8,128)(2,1)S(1)}, u32[]{:S(2)}, u32[]{:S(2)}) collective-permute-start(bf16[128,1024]{1,0:T(8,128)(2,1)} %get-tuple-element.24.refs_16_), channel_id=1, source_target_pairs={{0,2},{1,3},{2,4},{3,5},{4,6},{5,7},{6,8},{7,9},{8,10},{9,11},{10,... | collective-permute-start | bytes 786440 | tf_op jit(solution)/shard_map/ppermute | solution.py:85
  20.1 30.8 %collective-permute-start.26 = (bf16[128,1024]{1,0:T(8,128)(2,1)S(1)}, bf16[128,1024]{1,0:T(8,128)(2,1)S(1)}, u32[]{:S(2)}, u32[]{:S(2)}) collective-permute-start(bf16[128,1024]{1,0:T(8,128)(2,1)S(1)} %collective-permute-done.22.refs_24_), channel_id=1, source_target_pairs={{0,14},{1,15},{2,0},{3,1},{4,2},{5,3},{6,4},{7,5},{8,6},{9,7},{10,... | collective-permute-start | bytes 786440 | tf_op jit(solution)/shard_map/ppermute | solution.py:85
  23.6 24.1 %collective-permute-start.9 = (bf16[8,112,128]{2,1,0:T(8,128)(2,1)S(1)}, bf16[8,112,128]{2,1,0:T(8,128)(2,1)S(1)}, u32[]{:S(2)}, u32[]{:S(2)}) collective-permute-start(bf16[8,112,128]{2,1,0:T(8,128)(2,1)S(1)} %get-tuple-element.38), channel_id=1, source_target_pairs={{0,10},{1,11},{2,12},{3,13},{4,14},{5,15},{6,0},{7,1},{8,2},{9,3},... | collective-permute-start | bytes 688136 | tf_op jit(solution)/shard_map/ppermute | solution.py:85
  26.7 23.9 %collective-permute-start.8 = (bf16[8,112,128]{2,1,0:T(8,128)(2,1)S(1)}, bf16[8,112,128]{2,1,0:T(8,128)(2,1)S(1)}, u32[]{:S(2)}, u32[]{:S(2)}) collective-permute-start(bf16[8,112,128]{2,1,0:T(8,128)(2,1)S(1)} %get-tuple-element.39), channel_id=1, source_target_pairs={{0,6},{1,7},{2,8},{3,9},{4,10},{5,11},{6,12},{7,13},{8,14},{9,15},... | collective-permute-start | bytes 688136 | tf_op jit(solution)/shard_map/ppermute | solution.py:85
  36.5 20.6 %collective-permute-start.6 = (bf16[128,1024]{1,0:T(8,128)(2,1)S(1)}, bf16[128,1024]{1,0:T(8,128)(2,1)S(1)}, u32[]{:S(2)}, u32[]{:S(2)}) collective-permute-start(bf16[128,1024]{1,0:T(8,128)(2,1)S(1)} %collective-permute-done.2.refs_17_), channel_id=1, source_target_pairs={{0,2},{1,3},{2,4},{3,5},{4,6},{5,7},{6,8},{7,9},{8,10},{9,11},{10,... | collective-permute-start | bytes 786440 | tf_op jit(solution)/shard_map/ppermute | solution.py:85
  36.5 26.7 %collective-permute-start.7 = (bf16[128,1024]{1,0:T(8,128)(2,1)S(1)}, bf16[128,1024]{1,0:T(8,128)(2,1)S(1)}, u32[]{:S(2)}, u32[]{:S(2)}) collective-permute-start(bf16[128,1024]{1,0:T(8,128)(2,1)S(1)} %collective-permute-done.3.refs_23_), channel_id=1, source_target_pairs={{0,14},{1,15},{2,0},{3,1},{4,2},{5,3},{6,4},{7,5},{8,6},{9,7},{10,... | collective-permute-start | bytes 786440 | tf_op jit(solution)/shard_map/ppermute | solution.py:85
  47.8 15.4 %collective-permute-start.11 = (bf16[8,112,128]{2,1,0:T(8,128)(2,1)S(1)}, bf16[8,112,128]{2,1,0:T(8,128)(2,1)S(1)}, u32[]{:S(2)}, u32[]{:S(2)}) collective-permute-start(bf16[8,112,128]{2,1,0:T(8,128)(2,1)S(1)} %get-tuple-element.37), channel_id=1, source_target_pairs={{0,8},{1,9},{2,10},{3,11},{4,12},{5,13},{6,14},{7,15},{8,0},{9,1},... | collective-permute-start | bytes 688136 | tf_op jit(solution)/shard_map/ppermute | solution.py:85
  50.6 12.9 %collective-permute-start.12 = (bf16[8,112,128]{2,1,0:T(8,128)(2,1)S(1)}, bf16[8,112,128]{2,1,0:T(8,128)(2,1)S(1)}, u32[]{:S(2)}, u32[]{:S(2)}) collective-permute-start(bf16[8,112,128]{2,1,0:T(8,128)(2,1)S(1)} %get-tuple-element.44.refs_0_), channel_id=1, source_target_pairs={{0,1},{1,0},{2,3},{3,2},{4,5},{5,4},{6,7},{7,6},{8,9},{9,8},{10,11... | collective-permute-start | bytes 688136 | tf_op jit(solution)/shard_map/ppermute | solution.py:82
  50.9 13.8 %collective-permute-start.13 = (bf16[8,112,128]{2,1,0:T(8,128)(2,1)S(1)}, bf16[8,112,128]{2,1,0:T(8,128)(2,1)S(1)}, u32[]{:S(2)}, u32[]{:S(2)}) collective-permute-start(bf16[8,112,128]{2,1,0:T(8,128)(2,1)S(1)} %collective-permute-done.refs_1_), channel_id=1, source_target_pairs={{0,1},{1,0},{2,3},{3,2},{4,5},{5,4},{6,7},{7,6},{8,9},{9,8},{10,11... | collective-permute-start | bytes 688136 | tf_op jit(solution)/shard_map/ppermute | solution.py:82
  57.1 14.7 %collective-permute-start.23 = (bf16[128,1024]{1,0:T(8,128)(2,1)S(1)}, bf16[128,1024]{1,0:T(8,128)(2,1)S(1)}, u32[]{:S(2)}, u32[]{:S(2)}) collective-permute-start(bf16[128,1024]{1,0:T(8,128)(2,1)S(1)} %collective-permute-done.22.refs_24_), channel_id=1, source_target_pairs={{0,2},{1,3},{2,4},{3,5},{4,6},{5,7},{6,8},{7,9},{8,10},{9,11},{10,... | collective-permute-start | bytes 786440 | tf_op jit(solution)/shard_map/ppermute | solution.py:85
  63.2 11.6 %collective-permute-start.27 = (bf16[128,1024]{1,0:T(8,128)(2,1)S(1)}, bf16[128,1024]{1,0:T(8,128)(2,1)S(1)}, u32[]{:S(2)}, u32[]{:S(2)}) collective-permute-start(bf16[128,1024]{1,0:T(8,128)(2,1)S(1)} %collective-permute-done.26.refs_31_), channel_id=1, source_target_pairs={{0,14},{1,15},{2,0},{3,1},{4,2},{5,3},{6,4},{7,5},{8,6},{9,7},{10,... | collective-permute-start | bytes 786440 | tf_op jit(solution)/shard_map/ppermute | solution.py:85
  63.2 14.0 %collective-permute-start.19 = (bf16[8,112,128]{2,1,0:T(8,128)(2,1)S(1)}, bf16[8,112,128]{2,1,0:T(8,128)(2,1)S(1)}, u32[]{:S(2)}, u32[]{:S(2)}) collective-permute-start(bf16[8,112,128]{2,1,0:T(8,128)(2,1)S(1)} %collective-permute-done.1.refs_7_), channel_id=1, source_target_pairs={{0,1},{1,0},{2,3},{3,2},{4,5},{5,4},{6,7},{7,6},{8,9},{9,8},{10,11... | collective-permute-start | bytes 688136 | tf_op jit(solution)/shard_map/ppermute | solution.py:82
  63.5 14.0 %collective-permute-start.14 = (bf16[8,112,128]{2,1,0:T(8,128)(2,1)S(1)}, bf16[8,112,128]{2,1,0:T(8,128)(2,1)S(1)}, u32[]{:S(2)}, u32[]{:S(2)}) collective-permute-start(bf16[8,112,128]{2,1,0:T(8,128)(2,1)S(1)} %collective-permute-done.4.refs_2_), channel_id=1, source_target_pairs={{0,1},{1,0},{2,3},{3,2},{4,5},{5,4},{6,7},{7,6},{8,9},{9,8},{10,11... | collective-permute-start | bytes 688136 | tf_op jit(solution)/shard_map/ppermute | solution.py:82
  64.7 14.0 %collective-permute-start.10 = (bf16[128,1024]{1,0:T(8,128)(2,1)S(1)}, bf16[128,1024]{1,0:T(8,128)(2,1)S(1)}, u32[]{:S(2)}, u32[]{:S(2)}) collective-permute-start(bf16[128,1024]{1,0:T(8,128)(2,1)S(1)} %collective-permute-done.6.refs_18_), channel_id=1, source_target_pairs={{0,2},{1,3},{2,4},{3,5},{4,6},{5,7},{6,8},{7,9},{8,10},{9,11},{10,... | collective-permute-start | bytes 786440 | tf_op jit(solution)/shard_map/ppermute | solution.py:85
  71.8 11.2 %collective-permute-start.24 = (bf16[128,1024]{1,0:T(8,128)(2,1)S(1)}, bf16[128,1024]{1,0:T(8,128)(2,1)S(1)}, u32[]{:S(2)}, u32[]{:S(2)}) collective-permute-start(bf16[128,1024]{1,0:T(8,128)(2,1)S(1)} %collective-permute-done.23.refs_25_), channel_id=1, source_target_pairs={{0,2},{1,3},{2,4},{3,5},{4,6},{5,7},{6,8},{7,9},{8,10},{9,11},{10,... | collective-permute-start | bytes 786440 | tf_op jit(solution)/shard_map/ppermute | solution.py:85
  74.8 14.5 %collective-permute-start.28 = (bf16[128,1024]{1,0:T(8,128)(2,1)S(1)}, bf16[128,1024]{1,0:T(8,128)(2,1)S(1)}, u32[]{:S(2)}, u32[]{:S(2)}) collective-permute-start(bf16[128,1024]{1,0:T(8,128)(2,1)S(1)} %collective-permute-done.27.refs_30_), channel_id=1, source_target_pairs={{0,14},{1,15},{2,0},{3,1},{4,2},{5,3},{6,4},{7,5},{8,6},{9,7},{10,... | collective-permute-start | bytes 786440 | tf_op jit(solution)/shard_map/ppermute | solution.py:85
  77.5 10.2 %collective-permute-start.15 = (bf16[8,112,128]{2,1,0:T(8,128)(2,1)S(1)}, bf16[8,112,128]{2,1,0:T(8,128)(2,1)S(1)}, u32[]{:S(2)}, u32[]{:S(2)}) collective-permute-start(bf16[8,112,128]{2,1,0:T(8,128)(2,1)S(1)} %collective-permute-done.8.refs_3_), channel_id=1, source_target_pairs={{0,1},{1,0},{2,3},{3,2},{4,5},{5,4},{6,7},{7,6},{8,9},{9,8},{10,11... | collective-permute-start | bytes 688136 | tf_op jit(solution)/shard_map/ppermute | solution.py:82
  78.7 13.9 %collective-permute-start.17 = (bf16[8,112,128]{2,1,0:T(8,128)(2,1)S(1)}, bf16[8,112,128]{2,1,0:T(8,128)(2,1)S(1)}, u32[]{:S(2)}, u32[]{:S(2)}) collective-permute-start(bf16[8,112,128]{2,1,0:T(8,128)(2,1)S(1)} %collective-permute-done.9.refs_5_), channel_id=1, source_target_pairs={{0,1},{1,0},{2,3},{3,2},{4,5},{5,4},{6,7},{7,6},{8,9},{9,8},{10,11... | collective-permute-start | bytes 688136 | tf_op jit(solution)/shard_map/ppermute | solution.py:82
  82.8 10.1 %collective-permute-start.21 = (bf16[128,1024]{1,0:T(8,128)(2,1)S(1)}, bf16[128,1024]{1,0:T(8,128)(2,1)S(1)}, u32[]{:S(2)}, u32[]{:S(2)}) collective-permute-start(bf16[128,1024]{1,0:T(8,128)(2,1)S(1)} %collective-permute-done.7.refs_22_), channel_id=1, source_target_pairs={{0,14},{1,15},{2,0},{3,1},{4,2},{5,3},{6,4},{7,5},{8,6},{9,7},{10,... | collective-permute-start | bytes 786440 | tf_op jit(solution)/shard_map/ppermute | solution.py:85
  83.0 9.9 %collective-permute-start.25 = (bf16[128,1024]{1,0:T(8,128)(2,1)S(1)}, bf16[128,1024]{1,0:T(8,128)(2,1)S(1)}, u32[]{:S(2)}, u32[]{:S(2)}) collective-permute-start(bf16[128,1024]{1,0:T(8,128)(2,1)S(1)} %collective-permute-done.24.refs_26_), channel_id=1, source_target_pairs={{0,2},{1,3},{2,4},{3,5},{4,6},{5,7},{6,8},{7,9},{8,10},{9,11},{10,... | collective-permute-start | bytes 786440 | tf_op jit(solution)/shard_map/ppermute | solution.py:85
  87.7 10.1 %collective-permute-start.20 = (bf16[128,1024]{1,0:T(8,128)(2,1)S(1)}, bf16[128,1024]{1,0:T(8,128)(2,1)S(1)}, u32[]{:S(2)}, u32[]{:S(2)}) collective-permute-start(bf16[128,1024]{1,0:T(8,128)(2,1)S(1)} %collective-permute-done.10.refs_19_), channel_id=1, source_target_pairs={{0,2},{1,3},{2,4},{3,5},{4,6},{5,7},{6,8},{7,9},{8,10},{9,11},{10,... | collective-permute-start | bytes 786440 | tf_op jit(solution)/shard_map/ppermute | solution.py:85
  (9 other events, 55.7 us)

commit v3 on v2

v3 whole, which is shorter than its diff:
```python
import functools

import jax
import jax.numpy as jnp
from jax import lax
from jax.experimental import pallas as pl
from jax.experimental.pallas import tpu as pltpu
from jax.sharding import PartitionSpec as P

NB = 32
LANES = 128
VMEM = pl.BlockSpec(memory_space=pltpu.VMEM)
SMEM = pl.BlockSpec(memory_space=pltpu.SMEM)
STEP = 2


def position():
    me = lax.axis_index("ga")
    return me, lax.rem(me, 2), me // 2


def prepare(counts, k_minus_q, occupation, stored, keep, send, weights):
    me, x, z = position()
    count = counts[0]
    bands = weights.shape[0]
    rows = stored.shape[1]
    row = lax.broadcasted_iota(jnp.int32, (rows, LANES), 0)
    lane = lax.broadcasted_iota(jnp.int32, (rows, LANES), 1)
    true_row = ((row // NB) * 16 + me) * NB + row % NB
    for s in range(keep.shape[1] // LANES):
        for out, parity in ((keep, x), (send, 1 - x)):
            first = pl.multiple_of((2 * s + parity) * LANES, LANES)
            inside = (true_row < count) & (lane + first < count)
            block = stored[0, :, pl.ds(first, LANES)].astype(jnp.float32)
            out[:, s * LANES : (s + 1) * LANES] = jnp.where(inside, block, 0.0).astype(out.dtype)
    mine = occupation[pl.ds(pl.multiple_of(z * bands, bands), bands), :]
    k_point = lax.broadcasted_iota(jnp.int32, mine.shape, 1)
    mine = jnp.where(k_point == k_minus_q[0], mine, 0.0)
    for b in range(bands):
        weights[b] = jnp.sum(mine[b : b + 1])


def row_of(source, c, x_of):
    return (4 * c + source // 2) * LANES + (2 * lax.rem(source, 2) + x_of) * NB


def contract_most(n_z, *refs):
    own, other = refs[:2]
    rings = refs[2 : n_z + 1], refs[n_z + 1 : 2 * n_z]
    a_sorted, product, w_sorted = refs[2 * n_z :]
    _, x, z = position()
    _, bands, states, rows = a_sorted.shape
    half = n_z // 2

    for k in range(n_z):
        source = lax.rem(z + n_z - k, n_z)
        a_sorted[2 * source + x] = own[k * bands : (k + 1) * bands]
        a_sorted[2 * source + 1 - x] = other[k * bands : (k + 1) * bands]
        for ring, x_of in zip(rings, (x, 1 - x)):
            for c in range(rows // NB):
                to = pl.ds(pl.multiple_of(row_of(source, c, x_of), NB), NB)
                if k == half:
                    w_sorted[to, :] = jnp.zeros((NB, w_sorted.shape[1]), w_sorted.dtype)
                else:
                    w_sorted[to, :] = ring[k - (k > half)][c * NB : (c + 1) * NB, :]

    def some_bands(at, carry):
        b = at * STEP
        lhs = jnp.concatenate(
            [a_sorted[i, pl.ds(b, STEP)].reshape(STEP * states, LANES) for i in range(2 * n_z)], axis=1
        )
        product[at] = jnp.dot(lhs, w_sorted[...], preferred_element_type=jnp.float32)
        return carry

    lax.fori_loop(0, bands // STEP, some_bands, 0)


def contract_rest(n_z, weights, a_sorted, product, far_keep, far_recv, sigma, w_far):
    _, x, z = position()
    _, bands, states, rows = a_sorted.shape
    source = lax.rem(z + n_z // 2, n_z)
    cycles = rows // NB
    w_far[...] = jnp.zeros_like(w_far)
    for ref, x_of in ((far_keep, x), (far_recv, 1 - x)):
        for c in range(cycles):
            to = c * LANES + (2 * lax.rem(source, 2) + x_of) * NB
            w_far[pl.ds(pl.multiple_of(to, NB), NB), :] = ref[c * NB : (c + 1) * NB, :]

    def some_bands(at, total):
        b = at * STEP
        lhs = jnp.concatenate(
            [a_sorted[4 * c + source // 2, pl.ds(b, STEP)].reshape(STEP * states, LANES) for c in range(cycles)], axis=1
        )
        whole = product[at] + jnp.dot(lhs, w_far[...], preferred_element_type=jnp.float32)
        whole = whole.astype(jnp.bfloat16)
        for j in range(STEP):
            right = jnp.concatenate([a_sorted[2 * s + x, b + j] for s in range(n_z)], axis=1)
            pair = lax.dot_general(
                whole[j * states : (j + 1) * states],
                right,
                (((1,), (1,)), ((), ())),
                preferred_element_type=jnp.float32,
            )
            total = total - weights[b + j] * pair
        return total

    total = lax.fori_loop(0, bands // STEP, some_bands, jnp.zeros((states, states), jnp.float32))
    share = sigma.shape[1]
    for i in range(sigma.shape[0]):
        sigma[i] = total[i * share : (i + 1) * share]


def in_vmem(values):
    return [pltpu.with_memory_space_constraint(v, pltpu.VMEM) for v in values]


def pack(*refs):
    first = 0
    for ref in refs[:-1]:
        refs[-1][first : first + ref.shape[0]] = ref[...]
        first += ref.shape[0]


def packed(pieces):
    total = sum(piece.shape[0] for piece in pieces)
    return pl.pallas_call(
        pack,
        out_shape=jax.ShapeDtypeStruct((total, *pieces[0].shape[1:]), pieces[0].dtype),
        in_specs=[VMEM] * len(pieces),
        out_specs=VMEM,
    )(*in_vmem(pieces))


def on_device(elements, screened, counts, k_minus_q, occupation):
    _, n_band, n_state, g_slab = elements.shape
    groups = lax.axis_size("ga")
    n_z = groups // 2
    bands = n_band // n_z
    half_columns = screened.shape[2] // 2
    slab_shape = jax.ShapeDtypeStruct((bands, n_state, g_slab), jnp.bfloat16)
    half_shape = jax.ShapeDtypeStruct((g_slab, half_columns), jnp.bfloat16)
    limit = pltpu.CompilerParams(vmem_limit_bytes=20 * 1024 * 1024)

    def over_x(value):
        return lax.ppermute(value, "ga", [(i, i ^ 1) for i in range(groups)])

    def over_z(value, k):
        return lax.ppermute(value, "ga", [(i, (i + 2 * k) % groups) for i in range(groups)])

    keep, send, weights = pl.pallas_call(
        prepare,
        out_shape=[half_shape] * 2 + [jax.ShapeDtypeStruct((bands,), jnp.float32)],
        in_specs=[SMEM] * 2 + [VMEM] * 2,
        out_specs=[VMEM] * 2 + [SMEM],
    )(counts, k_minus_q, occupation.T, screened)

    slabs = elements[0].reshape(n_z, bands, n_state, g_slab)
    z = lax.axis_index("ga") // 2
    own = [lax.dynamic_index_in_dim(slabs, (z + k) % n_z, 0, keepdims=False) for k in range(n_z)]
    tie = lax.optimization_barrier
    opposite = [own[4][: bands // 2], own[4][bands // 2 :]]
    opposite = [over_z(opposite[0], 2), over_z(opposite[1], -2)]
    for k in (1, 7, 2, 6, 3, 5):
        own[k] = over_z(own[k], k)
    opposite = [over_z(opposite[0], 2), over_z(opposite[1], -2)]
    recv = over_x(send)
    ring_k, ring_r = [keep] + [None] * (n_z - 1), [recv] + [None] * (n_z - 1)
    own[1], own[7], own[2], own[6], own[3], own[5], opposite[0], opposite[1], ring_k[0], ring_r[0] = tie(
        (own[1], own[7], own[2], own[6], own[3], own[5], opposite[0], opposite[1], ring_k[0], ring_r[0])
    )
    own_all = packed(own[:4] + opposite + own[5:])
    other_all = over_x(own_all)
    ring_k[1], ring_k[7] = over_z(ring_k[0], 1), over_z(ring_k[0], -1)
    ring_r[1], ring_r[7] = over_z(ring_r[0], 1), over_z(ring_r[0], -1)
    ring_k[1], ring_k[7] = tie((ring_k[1], ring_k[7]))
    ring_r[1], ring_r[7] = tie((ring_r[1], ring_r[7]))
    ring_k[2], ring_k[6] = over_z(ring_k[1], 1), over_z(ring_k[7], -1)
    ring_r[2], ring_r[6] = over_z(ring_r[1], 1), over_z(ring_r[7], -1)
    ring_k[2], ring_k[6] = tie((ring_k[2], ring_k[6]))
    ring_r[2], ring_r[6] = tie((ring_r[2], ring_r[6]))
    ring_k[3], ring_k[5] = over_z(ring_k[2], 1), over_z(ring_k[6], -1)
    ring_r[3], ring_r[5] = over_z(ring_r[2], 1), over_z(ring_r[6], -1)
    ring_k[3], ring_k[5] = tie((ring_k[3], ring_k[5]))
    ring_r[3], ring_r[5], other_all = tie((ring_r[3], ring_r[5], other_all))
    ring_k[4], ring_r[4] = over_z(ring_k[3], 1), over_z(ring_r[5], -1)

    a_sorted, product = pl.pallas_call(
        functools.partial(contract_most, n_z),
        out_shape=[
            jax.ShapeDtypeStruct((groups, *slab_shape.shape), jnp.bfloat16),
            jax.ShapeDtypeStruct((bands // STEP, STEP * n_state, half_columns), jnp.float32),
        ],
        in_specs=[VMEM] * (2 * n_z),
        out_specs=[VMEM] * 2,
        scratch_shapes=[pltpu.VMEM((2 * half_columns, half_columns), jnp.bfloat16)],
        compiler_params=limit,
    )(*in_vmem([own_all, other_all] + ring_k[:4] + ring_k[5:] + ring_r[:4] + ring_r[5:]))
    shares = pl.pallas_call(
        functools.partial(contract_rest, n_z),
        out_shape=jax.ShapeDtypeStruct((groups, n_state // groups, n_state), jnp.float32),
        in_specs=[SMEM] + [VMEM] * 4,
        out_specs=VMEM,
        scratch_shapes=[pltpu.VMEM((half_columns // 2, half_columns), jnp.bfloat16)],
        compiler_params=limit,
    )(weights, *in_vmem([a_sorted, product, ring_k[4], ring_r[4]]))

    share = jnp.sum(lax.all_to_all(shares, "ga", 0, 0, tiled=True), axis=0)
    copies = jnp.broadcast_to(share[None], (lax.axis_size("pb"), *share.shape))
    return jnp.sum(lax.all_to_all(copies, "pb", 0, 0, tiled=True), axis=0)


def solution(mesh):
    return jax.shard_map(
        on_device,
        mesh=mesh,
        in_specs=(P("pb", None, None, "ga"), P("pb", "ga", None), P("pb"), P("pb"), P()),
        out_specs=P("ga", None),
        check_vma=False,
    )
```

time: 141 us -> 133 us (0.943)
  waiting for transfers between devices: 43.8 us -> 36.6 us
  Pallas kernels: 8.73 us -> 11.5 us
  starting transfers between devices: 47.9 us -> 45.3 us
    ppermute x9 -> x2, waiting for transfers between devices: 14.3 us -> 0.01 us  [over_x(): return lax.ppermute(value, 'ga', [(i, i ^ 1) for i in range(groups)])]
    ppermute x21 -> x24, waiting for transfers between devices: 29.6 us -> 36.6 us  [over_z(): lax.ppermute(value, 'ga', [(i, (i + 2 * k) % groups) for i in range(group...]
    ppermute x9 -> x2, starting transfers between devices: 6.22 us -> 2.89 us  [over_x(): return lax.ppermute(value, 'ga', [(i, i ^ 1) for i in range(groups)])]
    pallas_call x2 -> x4, Pallas kernels: 8.73 us -> 11.5 us  [the longest x1 5.03 us: on_device(): pl.pallas_call(functools.partial(contract_most, n_z), out_shape=[jax.Shap...]
    ppermute x21 -> x24, starting transfers between devices: 41.6 us -> 42.4 us  [over_z(): lax.ppermute(value, 'ga', [(i, (i + 2 * k) % groups) for i in range(group...]
  transfers between devices with their start and end apart: 30 -> 26, of which waited for: 11 -> 16; matrix products, arithmetic and copies ran while one was open for 1% -> 1% of each run, Pallas kernels for 2% -> 5%
where the time goes in v3:
time: 133 us
  starting transfers between devices  45.3 us (34%)
  waiting for transfers between devices  36.6 us (28%)
  blocking collectives  33.6 us (25%)
  Pallas kernels  11.5 us (9%)
  local copies, waits for them, and re-layouts  4.08 us (3%)
  between operations  1.41 us (1%)
    ppermute x24, starting transfers between devices, over_z(): lax.ppermute(value, 'ga', [(i, (i + 2 * k) % groups) for i in range(group...  42.4 us
    ppermute x24, waiting for transfers between devices, over_z(): lax.ppermute(value, 'ga', [(i, (i + 2 * k) % groups) for i in range(group...  36.6 us
    all_to_all x1, blocking collectives, on_device(): return jnp.sum(lax.all_to_all(copies, 'pb', 0, 0, tiled=True), axis=0)  17.3 us
    all_to_all x1, blocking collectives, on_device(): share = jnp.sum(lax.all_to_all(shares, 'ga', 0, 0, tiled=True), axis=0)  16.4 us
    pallas_call x1, Pallas kernels, on_device(): pl.pallas_call(functools.partial(contract_most, n_z), out_shape=[jax.Shap...  5.03 us
    pallas_call x1, Pallas kernels, on_device(): pl.pallas_call(functools.partial(contract_rest, n_z), out_shape=jax.Shape...  2.92 us
    ppermute x2, starting transfers between devices, over_x(): return lax.ppermute(value, 'ga', [(i, i ^ 1) for i in range(groups)])  2.89 us
  transfers between devices with their start and end apart: 26, of which 16 were waited for; matrix products, arithmetic and copies ran while one was open for 1% of the time, Pallas kernels for 5%

profile of v3, /device:TPU:1, one launch (start us, length us, event | category | flops | bytes accessed | tf_op | source)
XLA Modules:
  0.0 133.2 jit_solution(1177531302034637532)
XLA Ops:
  1.6 2.5 %collective-permute-start = (bf16[8,112,128]{2,1,0:T(8,128)(2,1)S(1)}, bf16[8,112,128]{2,1,0:T(8,128)(2,1)S(1)}, u32[]{:S(2)}, u32[]{:S(2)}) collective-permute-start(bf16[8,112,128]{2,1,0:T(8,128)(2,1)S(1)} %get-tuple-element.68), channel_id=1, source_target_pairs={{0,2},{1,3},{2,4},{3,5},{4,6},{5,7},{6,8},{7,9},{8,10},{9,11},{10,... | collective-permute-start | bytes 688136 | tf_op jit(solution)/shard_map/ppermute | solution.py:148
  4.1 4.0 %collective-permute-start.1 = (bf16[8,112,128]{2,1,0:T(8,128)(2,1)S(1)}, bf16[8,112,128]{2,1,0:T(8,128)(2,1)S(1)}, u32[]{:S(2)}, u32[]{:S(2)}) collective-permute-start(bf16[8,112,128]{2,1,0:T(8,128)(2,1)S(1)} %get-tuple-element.67), channel_id=1, source_target_pairs={{0,14},{1,15},{2,0},{3,1},{4,2},{5,3},{6,4},{7,5},{8,6},{9,7},{10,... | collective-permute-start | bytes 688136 | tf_op jit(solution)/shard_map/ppermute | solution.py:148
  9.2 3.6 %collective-permute-start.8 = (bf16[4,112,128]{2,1,0:T(8,128)(2,1)S(1)}, bf16[4,112,128]{2,1,0:T(8,128)(2,1)S(1)}, u32[]{:S(2)}, u32[]{:S(2)}) collective-permute-start(bf16[4,112,128]{2,1,0:T(8,128)(2,1)S(1)} %get-tuple-element.61), channel_id=1, source_target_pairs={{0,12},{1,13},{2,14},{3,15},{4,0},{5,1},{6,2},{7,3},{8,4},{9,5},{1... | collective-permute-start | bytes 344072 | tf_op jit(solution)/shard_map/ppermute | solution.py:148
  13.4 4.3 %collective-permute-done.6 = bf16[4,112,128]{2,1,0:T(8,128)(2,1)S(1)} collective-permute-done((bf16[4,112,128]{2,1,0:T(8,128)(2,1)S(1)}, bf16[4,112,128]{2,1,0:T(8,128)(2,1)S(1)}, u32[]{:S(2)}, u32[]{:S(2)}) %collective-permute-start.6) | collective-permute-done | bytes 114720 | tf_op jit(solution)/shard_map/ppermute | solution.py:148
  19.7 2.2 %shard_map.55 = (bf16[128,1024]{1,0:T(8,128)(2,1)}, bf16[128,1024]{1,0:T(8,128)(2,1)}, f32[8]{0:T(128)}) custom-call(s32[1]{0:T(128)S(6)} %copy.8.counts, s32[1]{0:T(128)S(6)} %copy.9.k_minus_q, f32[64,576]{1,0:T(8,128)} %bitcast.22, bf16[1,128,2048]{2,1,0:T(8,128)(2,1)} %stored.1), custom_call_target="tpu_custom_call" | custom-call | tf_op jit(solution)/shard_map/pallas_call | solution.py:150
  24.9 2.8 %collective-permute-start.5 = (bf16[8,112,128]{2,1,0:T(8,128)(2,1)S(1)}, bf16[8,112,128]{2,1,0:T(8,128)(2,1)S(1)}, u32[]{:S(2)}, u32[]{:S(2)}) collective-permute-start(bf16[8,112,128]{2,1,0:T(8,128)(2,1)S(1)} %get-tuple-element.63), channel_id=1, source_target_pairs={{0,10},{1,11},{2,12},{3,13},{4,14},{5,15},{6,0},{7,1},{8,2},{9,3},... | collective-permute-start | bytes 688136 | tf_op jit(solution)/shard_map/ppermute | solution.py:148
  29.3 2.6 %collective-permute-start.9 = (bf16[4,112,128]{2,1,0:T(8,128)(2,1)S(1)}, bf16[4,112,128]{2,1,0:T(8,128)(2,1)S(1)}, u32[]{:S(2)}, u32[]{:S(2)}) collective-permute-start(bf16[4,112,128]{2,1,0:T(8,128)(2,1)S(1)} %collective-permute-done.8), channel_id=1, source_target_pairs={{0,12},{1,13},{2,14},{3,15},{4,0},{5,1},{6,2},{7,3},{8,4},{9,5},{1... | collective-permute-start | bytes 344072 | tf_op jit(solution)/shard_map/ppermute | solution.py:148
  31.9 9.3 %collective-permute-done.4.refs_3_ = bf16[8,112,128]{2,1,0:T(8,128)(2,1)S(1)} collective-permute-done((bf16[8,112,128]{2,1,0:T(8,128)(2,1)S(1)}, bf16[8,112,128]{2,1,0:T(8,128)(2,1)S(1)}, u32[]{:S(2)}, u32[]{:S(2)}) %collective-permute-start.4) | collective-permute-done | bytes 229408 | tf_op jit(solution)/shard_map/ppermute | solution.py:148
  41.2 2.5 %collective-permute-done.5.refs_6_ = bf16[8,112,128]{2,1,0:T(8,128)(2,1)S(1)} collective-permute-done((bf16[8,112,128]{2,1,0:T(8,128)(2,1)S(1)}, bf16[8,112,128]{2,1,0:T(8,128)(2,1)S(1)}, u32[]{:S(2)}, u32[]{:S(2)}) %collective-permute-start.5) | collective-permute-done | bytes 229408 | tf_op jit(solution)/shard_map/ppermute | solution.py:148
  43.7 2.6 %collective-permute-done.7.refs_4_ = bf16[4,112,128]{2,1,0:T(8,128)(2,1)S(1)} collective-permute-done((bf16[4,112,128]{2,1,0:T(8,128)(2,1)S(1)}, bf16[4,112,128]{2,1,0:T(8,128)(2,1)S(1)}, u32[]{:S(2)}, u32[]{:S(2)}) %collective-permute-start.7) | collective-permute-done | bytes 114720 | tf_op jit(solution)/shard_map/ppermute | solution.py:148
  49.3 3.3 %collective-permute-start.18 = (bf16[128,1024]{1,0:T(8,128)(2,1)S(1)}, bf16[128,1024]{1,0:T(8,128)(2,1)S(1)}, u32[]{:S(2)}, u32[]{:S(2)}) collective-permute-start(bf16[128,1024]{1,0:T(8,128)(2,1)S(1)} %copy-done.1), channel_id=1, source_target_pairs={{0,2},{1,3},{2,4},{3,5},{4,6},{5,7},{6,8},{7,9},{8,10},{9,11},{10,... | collective-permute-start | bytes 786440 | tf_op jit(solution)/shard_map/ppermute | solution.py:148
  56.0 2.2 %collective-permute-done.19.refs_8_ = bf16[128,1024]{1,0:T(8,128)(2,1)S(1)} collective-permute-done((bf16[128,1024]{1,0:T(8,128)(2,1)S(1)}, bf16[128,1024]{1,0:T(8,128)(2,1)S(1)}, u32[]{:S(2)}, u32[]{:S(2)}) %collective-permute-start.19) | collective-permute-done | bytes 262176 | tf_op jit(solution)/shard_map/ppermute | solution.py:148
  58.3 2.5 %collective-permute-start.21 = (bf16[128,1024]{1,0:T(8,128)(2,1)S(1)}, bf16[128,1024]{1,0:T(8,128)(2,1)S(1)}, u32[]{:S(2)}, u32[]{:S(2)}) collective-permute-start(bf16[128,1024]{1,0:T(8,128)(2,1)S(1)} %collective-permute-done.19.refs_8_), channel_id=1, source_target_pairs={{0,14},{1,15},{2,0},{3,1},{4,2},{5,3},{6,4},{7,5},{8,6},{9,7},{10,... | collective-permute-start | bytes 786440 | tf_op jit(solution)/shard_map/ppermute | solution.py:148
  61.4 1.9 %collective-permute-done.12.refs_15_ = bf16[128,1024]{1,0:T(8,128)(2,1)S(1)} collective-permute-done((bf16[128,1024]{1,0:T(8,128)(2,1)S(1)}, bf16[128,1024]{1,0:T(8,128)(2,1)S(1)}, u32[]{:S(2)}, u32[]{:S(2)}) %collective-permute-start.12) | collective-permute-done | bytes 262176 | tf_op jit(solution)/shard_map/ppermute | solution.py:148
  63.6 2.4 %collective-permute-start.14 = (bf16[128,1024]{1,0:T(8,128)(2,1)S(1)}, bf16[128,1024]{1,0:T(8,128)(2,1)S(1)}, u32[]{:S(2)}, u32[]{:S(2)}) collective-permute-start(bf16[128,1024]{1,0:T(8,128)(2,1)S(1)} %collective-permute-done.12.refs_15_), channel_id=1, source_target_pairs={{0,14},{1,15},{2,0},{3,1},{4,2},{5,3},{6,4},{7,5},{8,6},{9,7},{10,... | collective-permute-start | bytes 786440 | tf_op jit(solution)/shard_map/ppermute | solution.py:148
  69.6 2.1 %collective-permute-start.23 = (bf16[128,1024]{1,0:T(8,128)(2,1)S(1)}, bf16[128,1024]{1,0:T(8,128)(2,1)S(1)}, u32[]{:S(2)}, u32[]{:S(2)}) collective-permute-start(bf16[128,1024]{1,0:T(8,128)(2,1)S(1)} %collective-permute-done.21.refs_7_), channel_id=1, source_target_pairs={{0,14},{1,15},{2,0},{3,1},{4,2},{5,3},{6,4},{7,5},{8,6},{9,7},{10,... | collective-permute-start | bytes 786440 | tf_op jit(solution)/shard_map/ppermute | solution.py:148
  72.7 1.9 %collective-permute-done.14.refs_14_ = bf16[128,1024]{1,0:T(8,128)(2,1)S(1)} collective-permute-done((bf16[128,1024]{1,0:T(8,128)(2,1)S(1)}, bf16[128,1024]{1,0:T(8,128)(2,1)S(1)}, u32[]{:S(2)}, u32[]{:S(2)}) %collective-permute-start.14) | collective-permute-done | bytes 262176 | tf_op jit(solution)/shard_map/ppermute | solution.py:148
  78.3 1.9 %collective-permute-done.23.refs_6_ = bf16[128,1024]{1,0:T(8,128)(2,1)S(1)} collective-permute-done((bf16[128,1024]{1,0:T(8,128)(2,1)S(1)}, bf16[128,1024]{1,0:T(8,128)(2,1)S(1)}, u32[]{:S(2)}, u32[]{:S(2)}) %collective-permute-start.23) | collective-permute-done | bytes 262176 | tf_op jit(solution)/shard_map/ppermute | solution.py:148
  83.9 1.9 %collective-permute-done.16.refs_13_ = bf16[128,1024]{1,0:T(8,128)(2,1)S(1)} collective-permute-done((bf16[128,1024]{1,0:T(8,128)(2,1)S(1)}, bf16[128,1024]{1,0:T(8,128)(2,1)S(1)}, u32[]{:S(2)}, u32[]{:S(2)}) %collective-permute-start.16) | collective-permute-done | bytes 262176 | tf_op jit(solution)/shard_map/ppermute | solution.py:148
  85.8 3.6 %collective-permute-start.25 = (bf16[128,1024]{1,0:T(8,128)(2,1)S(1)}, bf16[128,1024]{1,0:T(8,128)(2,1)S(1)}, u32[]{:S(2)}, u32[]{:S(2)}) collective-permute-start(bf16[128,1024]{1,0:T(8,128)(2,1)S(1)} %collective-permute-done.16.refs_13_), channel_id=1, source_target_pairs={{0,14},{1,15},{2,0},{3,1},{4,2},{5,3},{6,4},{7,5},{8,6},{9,7},{10,... | collective-permute-start | bytes 786440 | tf_op jit(solution)/shard_map/ppermute | solution.py:148
  90.9 5.0 %shard_map.57 = (bf16[16,8,112,128]{3,2,1,0:T(8,128)(2,1)S(1)}, f32[4,224,1024]{2,1,0:T(8,128)S(1)}) custom-call(bf16[64,112,128]{2,1,0:T(8,128)(2,1)S(1)} %copy-done, bf16[64,112,128]{2,1,0:T(8,128)(2,1)S(1)} %collective-permute-done.17.refs_1_, bf16[128,1024]{1,0:T(8,128)(2,1)S(1)} %copy-done.1, bf16[128,1024]{1,0:T(8,128)(2,1)S(1)} %collective-permute-done.18.refs_3_, ...), custom_call_target="tpu_custom_call" | custom-call | tf_op jit(solution)/shard_map/pallas_call | solution.py:187
  96.0 2.9 %shard_map.58 = f32[16,7,112]{2,1,0:T(8,128)S(1)} custom-call(f32[8]{0:T(128)S(1)} %copy-done.2, bf16[16,8,112,128]{3,2,1,0:T(8,128)(2,1)S(1)} %get-tuple-element.59.a_sorted, f32[4,224,1024]{2,1,0:T(8,128)S(1)} %get-tuple-element.60.product, bf16[128,1024]{1,0:T(8,128)(2,1)S(1)} %collective-permute-done.24.far_keep, ...), custom_call_target="tpu_custom_call" | custom-call | tf_op jit(solution)/shard_map/pallas_call | solution.py:198
  98.9 16.4 %all_to_all.10 = f32[16,7,112]{2,1,0:T(8,128)S(1)} all-to-all(f32[16,7,112]{2,1,0:T(8,128)S(1)} %shard_map.58), channel_id=1, replica_groups=mesh['pb'=16,'ga'=16] {'ga'}, dimensions={0} | all-to-all | bytes 100352 | tf_op jit(solution)/shard_map/all_to_all | solution.py:207
  115.3 17.3 %all_to_all.11 = f32[16,7,112]{2,1,0:T(8,128)S(1)} all-to-all(f32[16,7,112]{2,1,0:T(8,128)S(1)} %broadcast_in_dim.2), channel_id=1, replica_groups=mesh['pb'=16,'ga'=16] {'pb'}, dimensions={0} | all-to-all | bytes 100352 | tf_op jit(solution)/shard_map/all_to_all | solution.py:209
  (45 shorter events, 30.2 us)
Async XLA Ops:
  1.6 21.6 %collective-permute-start = (bf16[8,112,128]{2,1,0:T(8,128)(2,1)S(1)}, bf16[8,112,128]{2,1,0:T(8,128)(2,1)S(1)}, u32[]{:S(2)}, u32[]{:S(2)}) collective-permute-start(bf16[8,112,128]{2,1,0:T(8,128)(2,1)S(1)} %get-tuple-element.68), channel_id=1, source_target_pairs={{0,2},{1,3},{2,4},{3,5},{4,6},{5,7},{6,8},{7,9},{8,10},{9,11},{10,... | collective-permute-start | bytes 688136 | tf_op jit(solution)/shard_map/ppermute | solution.py:148
  4.1 20.7 %collective-permute-start.1 = (bf16[8,112,128]{2,1,0:T(8,128)(2,1)S(1)}, bf16[8,112,128]{2,1,0:T(8,128)(2,1)S(1)}, u32[]{:S(2)}, u32[]{:S(2)}) collective-permute-start(bf16[8,112,128]{2,1,0:T(8,128)(2,1)S(1)} %get-tuple-element.67), channel_id=1, source_target_pairs={{0,14},{1,15},{2,0},{3,1},{4,2},{5,3},{6,4},{7,5},{8,6},{9,7},{10,... | collective-permute-start | bytes 688136 | tf_op jit(solution)/shard_map/ppermute | solution.py:148
  9.1 8.5 %collective-permute-start.6 = (bf16[4,112,128]{2,1,0:T(8,128)(2,1)S(1)}, bf16[4,112,128]{2,1,0:T(8,128)(2,1)S(1)}, u32[]{:S(2)}, u32[]{:S(2)}) collective-permute-start(bf16[4,112,128]{2,1,0:T(8,128)(2,1)S(1)} %get-tuple-element.62), channel_id=1, source_target_pairs={{0,4},{1,5},{2,6},{3,7},{4,8},{5,9},{6,10},{7,11},{8,12},{9,13},{1... | collective-permute-start | bytes 344072 | tf_op jit(solution)/shard_map/ppermute | solution.py:148
  9.2 12.6 %collective-permute-start.8 = (bf16[4,112,128]{2,1,0:T(8,128)(2,1)S(1)}, bf16[4,112,128]{2,1,0:T(8,128)(2,1)S(1)}, u32[]{:S(2)}, u32[]{:S(2)}) collective-permute-start(bf16[4,112,128]{2,1,0:T(8,128)(2,1)S(1)} %get-tuple-element.61), channel_id=1, source_target_pairs={{0,12},{1,13},{2,14},{3,15},{4,0},{5,1},{6,2},{7,3},{8,4},{9,5},{1... | collective-permute-start | bytes 344072 | tf_op jit(solution)/shard_map/ppermute | solution.py:148
  12.8 14.9 %collective-permute-start.2 = (bf16[8,112,128]{2,1,0:T(8,128)(2,1)S(1)}, bf16[8,112,128]{2,1,0:T(8,128)(2,1)S(1)}, u32[]{:S(2)}, u32[]{:S(2)}) collective-permute-start(bf16[8,112,128]{2,1,0:T(8,128)(2,1)S(1)} %get-tuple-element.66), channel_id=1, source_target_pairs={{0,4},{1,5},{2,6},{3,7},{4,8},{5,9},{6,10},{7,11},{8,12},{9,13},{1... | collective-permute-start | bytes 688136 | tf_op jit(solution)/shard_map/ppermute | solution.py:148
  17.7 11.6 %collective-permute-start.3 = (bf16[8,112,128]{2,1,0:T(8,128)(2,1)S(1)}, bf16[8,112,128]{2,1,0:T(8,128)(2,1)S(1)}, u32[]{:S(2)}, u32[]{:S(2)}) collective-permute-start(bf16[8,112,128]{2,1,0:T(8,128)(2,1)S(1)} %get-tuple-element.65), channel_id=1, source_target_pairs={{0,12},{1,13},{2,14},{3,15},{4,0},{5,1},{6,2},{7,3},{8,4},{9,5},{1... | collective-permute-start | bytes 688136 | tf_op jit(solution)/shard_map/ppermute | solution.py:148
  21.9 24.5 %collective-permute-start.10 = (bf16[128,1024]{1,0:T(8,128)(2,1)}, bf16[128,1024]{1,0:T(8,128)(2,1)S(1)}, u32[]{:S(2)}, u32[]{:S(2)}) collective-permute-start(bf16[128,1024]{1,0:T(8,128)(2,1)} %get-tuple-element.35), channel_id=1, source_target_pairs={{0,1},{1,0},{2,3},{3,2},{4,5},{5,4},{6,7},{7,6},{8,9},{9,8},{10,11... | collective-permute-start | bytes 786440 | tf_op jit(solution)/shard_map/ppermute | solution.py:145
  23.2 18.0 %collective-permute-start.4 = (bf16[8,112,128]{2,1,0:T(8,128)(2,1)S(1)}, bf16[8,112,128]{2,1,0:T(8,128)(2,1)S(1)}, u32[]{:S(2)}, u32[]{:S(2)}) collective-permute-start(bf16[8,112,128]{2,1,0:T(8,128)(2,1)S(1)} %get-tuple-element.64), channel_id=1, source_target_pairs={{0,6},{1,7},{2,8},{3,9},{4,10},{5,11},{6,12},{7,13},{8,14},{9,15},... | collective-permute-start | bytes 688136 | tf_op jit(solution)/shard_map/ppermute | solution.py:148
  24.9 18.8 %collective-permute-start.5 = (bf16[8,112,128]{2,1,0:T(8,128)(2,1)S(1)}, bf16[8,112,128]{2,1,0:T(8,128)(2,1)S(1)}, u32[]{:S(2)}, u32[]{:S(2)}) collective-permute-start(bf16[8,112,128]{2,1,0:T(8,128)(2,1)S(1)} %get-tuple-element.63), channel_id=1, source_target_pairs={{0,10},{1,11},{2,12},{3,13},{4,14},{5,15},{6,0},{7,1},{8,2},{9,3},... | collective-permute-start | bytes 688136 | tf_op jit(solution)/shard_map/ppermute | solution.py:148
  27.7 18.7 %collective-permute-start.7 = (bf16[4,112,128]{2,1,0:T(8,128)(2,1)S(1)}, bf16[4,112,128]{2,1,0:T(8,128)(2,1)S(1)}, u32[]{:S(2)}, u32[]{:S(2)}) collective-permute-start(bf16[4,112,128]{2,1,0:T(8,128)(2,1)S(1)} %collective-permute-done.6), channel_id=1, source_target_pairs={{0,4},{1,5},{2,6},{3,7},{4,8},{5,9},{6,10},{7,11},{8,12},{9,13},{1... | collective-permute-start | bytes 344072 | tf_op jit(solution)/shard_map/ppermute | solution.py:148
  29.3 17.0 %collective-permute-start.9 = (bf16[4,112,128]{2,1,0:T(8,128)(2,1)S(1)}, bf16[4,112,128]{2,1,0:T(8,128)(2,1)S(1)}, u32[]{:S(2)}, u32[]{:S(2)}) collective-permute-start(bf16[4,112,128]{2,1,0:T(8,128)(2,1)S(1)} %collective-permute-done.8), channel_id=1, source_target_pairs={{0,12},{1,13},{2,14},{3,15},{4,0},{5,1},{6,2},{7,3},{8,4},{9,5},{1... | collective-permute-start | bytes 344072 | tf_op jit(solution)/shard_map/ppermute | solution.py:148
  47.7 38.1 %collective-permute-start.17 = (bf16[64,112,128]{2,1,0:T(8,128)(2,1)}, bf16[64,112,128]{2,1,0:T(8,128)(2,1)S(1)}, u32[]{:S(2)}, u32[]{:S(2)}) collective-permute-start(bf16[64,112,128]{2,1,0:T(8,128)(2,1)} %shard_map.56.refs_0_), channel_id=1, source_target_pairs={{0,1},{1,0},{2,3},{3,2},{4,5},{5,4},{6,7},{7,6},{8,9},{9,8},{10,11... | collective-permute-start | bytes 5505032 | tf_op jit(solution)/shard_map/ppermute | solution.py:145
  52.6 8.8 %collective-permute-start.11 = (bf16[128,1024]{1,0:T(8,128)(2,1)S(1)}, bf16[128,1024]{1,0:T(8,128)(2,1)S(1)}, u32[]{:S(2)}, u32[]{:S(2)}) collective-permute-start(bf16[128,1024]{1,0:T(8,128)(2,1)S(1)} %collective-permute-done.10.refs_9_), channel_id=1, source_target_pairs={{0,2},{1,3},{2,4},{3,5},{4,6},{5,7},{6,8},{7,9},{8,10},{9,11},{10,... | collective-permute-start | bytes 786440 | tf_op jit(solution)/shard_map/ppermute | solution.py:148
  54.1 9.2 %collective-permute-start.12 = (bf16[128,1024]{1,0:T(8,128)(2,1)S(1)}, bf16[128,1024]{1,0:T(8,128)(2,1)S(1)}, u32[]{:S(2)}, u32[]{:S(2)}) collective-permute-start(bf16[128,1024]{1,0:T(8,128)(2,1)S(1)} %collective-permute-done.10.refs_9_), channel_id=1, source_target_pairs={{0,14},{1,15},{2,0},{3,1},{4,2},{5,3},{6,4},{7,5},{8,6},{9,7},{10,... | collective-permute-start | bytes 786440 | tf_op jit(solution)/shard_map/ppermute | solution.py:148
  58.2 9.6 %collective-permute-start.20 = (bf16[128,1024]{1,0:T(8,128)(2,1)S(1)}, bf16[128,1024]{1,0:T(8,128)(2,1)S(1)}, u32[]{:S(2)}, u32[]{:S(2)}) collective-permute-start(bf16[128,1024]{1,0:T(8,128)(2,1)S(1)} %collective-permute-done.18.refs_3_), channel_id=1, source_target_pairs={{0,2},{1,3},{2,4},{3,5},{4,6},{5,7},{6,8},{7,9},{8,10},{9,11},{10,... | collective-permute-start | bytes 786440 | tf_op jit(solution)/shard_map/ppermute | solution.py:148
  58.3 10.6 %collective-permute-start.21 = (bf16[128,1024]{1,0:T(8,128)(2,1)S(1)}, bf16[128,1024]{1,0:T(8,128)(2,1)S(1)}, u32[]{:S(2)}, u32[]{:S(2)}) collective-permute-start(bf16[128,1024]{1,0:T(8,128)(2,1)S(1)} %collective-permute-done.19.refs_8_), channel_id=1, source_target_pairs={{0,14},{1,15},{2,0},{3,1},{4,2},{5,3},{6,4},{7,5},{8,6},{9,7},{10,... | collective-permute-start | bytes 786440 | tf_op jit(solution)/shard_map/ppermute | solution.py:148
  63.3 9.3 %collective-permute-start.13 = (bf16[128,1024]{1,0:T(8,128)(2,1)S(1)}, bf16[128,1024]{1,0:T(8,128)(2,1)S(1)}, u32[]{:S(2)}, u32[]{:S(2)}) collective-permute-start(bf16[128,1024]{1,0:T(8,128)(2,1)S(1)} %collective-permute-done.11.refs_10_), channel_id=1, source_target_pairs={{0,2},{1,3},{2,4},{3,5},{4,6},{5,7},{6,8},{7,9},{8,10},{9,11},{10,... | collective-permute-start | bytes 786440 | tf_op jit(solution)/shard_map/ppermute | solution.py:148
  63.6 10.9 %collective-permute-start.14 = (bf16[128,1024]{1,0:T(8,128)(2,1)S(1)}, bf16[128,1024]{1,0:T(8,128)(2,1)S(1)}, u32[]{:S(2)}, u32[]{:S(2)}) collective-permute-start(bf16[128,1024]{1,0:T(8,128)(2,1)S(1)} %collective-permute-done.12.refs_15_), channel_id=1, source_target_pairs={{0,14},{1,15},{2,0},{3,1},{4,2},{5,3},{6,4},{7,5},{8,6},{9,7},{10,... | collective-permute-start | bytes 786440 | tf_op jit(solution)/shard_map/ppermute | solution.py:148
  68.9 9.3 %collective-permute-start.22 = (bf16[128,1024]{1,0:T(8,128)(2,1)S(1)}, bf16[128,1024]{1,0:T(8,128)(2,1)S(1)}, u32[]{:S(2)}, u32[]{:S(2)}) collective-permute-start(bf16[128,1024]{1,0:T(8,128)(2,1)S(1)} %collective-permute-done.20.refs_4_), channel_id=1, source_target_pairs={{0,2},{1,3},{2,4},{3,5},{4,6},{5,7},{6,8},{7,9},{8,10},{9,11},{10,... | collective-permute-start | bytes 786440 | tf_op jit(solution)/shard_map/ppermute | solution.py:148
  69.6 10.6 %collective-permute-start.23 = (bf16[128,1024]{1,0:T(8,128)(2,1)S(1)}, bf16[128,1024]{1,0:T(8,128)(2,1)S(1)}, u32[]{:S(2)}, u32[]{:S(2)}) collective-permute-start(bf16[128,1024]{1,0:T(8,128)(2,1)S(1)} %collective-permute-done.21.refs_7_), channel_id=1, source_target_pairs={{0,14},{1,15},{2,0},{3,1},{4,2},{5,3},{6,4},{7,5},{8,6},{9,7},{10,... | collective-permute-start | bytes 786440 | tf_op jit(solution)/shard_map/ppermute | solution.py:148
  74.5 9.3 %collective-permute-start.15 = (bf16[128,1024]{1,0:T(8,128)(2,1)S(1)}, bf16[128,1024]{1,0:T(8,128)(2,1)S(1)}, u32[]{:S(2)}, u32[]{:S(2)}) collective-permute-start(bf16[128,1024]{1,0:T(8,128)(2,1)S(1)} %collective-permute-done.13.refs_11_), channel_id=1, source_target_pairs={{0,2},{1,3},{2,4},{3,5},{4,6},{5,7},{6,8},{7,9},{8,10},{9,11},{10,... | collective-permute-start | bytes 786440 | tf_op jit(solution)/shard_map/ppermute | solution.py:148
  76.4 9.4 %collective-permute-start.16 = (bf16[128,1024]{1,0:T(8,128)(2,1)S(1)}, bf16[128,1024]{1,0:T(8,128)(2,1)S(1)}, u32[]{:S(2)}, u32[]{:S(2)}) collective-permute-start(bf16[128,1024]{1,0:T(8,128)(2,1)S(1)} %collective-permute-done.14.refs_14_), channel_id=1, source_target_pairs={{0,14},{1,15},{2,0},{3,1},{4,2},{5,3},{6,4},{7,5},{8,6},{9,7},{10,... | collective-permute-start | bytes 786440 | tf_op jit(solution)/shard_map/ppermute | solution.py:148
  80.2 15.8 %collective-permute-start.24 = (bf16[128,1024]{1,0:T(8,128)(2,1)S(1)}, bf16[128,1024]{1,0:T(8,128)(2,1)S(1)}, u32[]{:S(2)}, u32[]{:S(2)}) collective-permute-start(bf16[128,1024]{1,0:T(8,128)(2,1)S(1)} %collective-permute-done.22.refs_5_), channel_id=1, source_target_pairs={{0,2},{1,3},{2,4},{3,5},{4,6},{5,7},{6,8},{7,9},{8,10},{9,11},{10,... | collective-permute-start | bytes 786440 | tf_op jit(solution)/shard_map/ppermute | solution.py:148
  85.8 10.2 %collective-permute-start.25 = (bf16[128,1024]{1,0:T(8,128)(2,1)S(1)}, bf16[128,1024]{1,0:T(8,128)(2,1)S(1)}, u32[]{:S(2)}, u32[]{:S(2)}) collective-permute-start(bf16[128,1024]{1,0:T(8,128)(2,1)S(1)} %collective-permute-done.16.refs_13_), channel_id=1, source_target_pairs={{0,14},{1,15},{2,0},{3,1},{4,2},{5,3},{6,4},{7,5},{8,6},{9,7},{10,... | collective-permute-start | bytes 786440 | tf_op jit(solution)/shard_map/ppermute | solution.py:148
  (5 other events, 66.3 us)

commit v4 on v3

--- a/solution.py
+++ b/solution.py
@@ -125,9 +125,10 @@
     total = sum(piece.shape[0] for piece in pieces)
     return pl.pallas_call(
         pack,
-        out_shape=jax.ShapeDtypeStruct((total, *pieces[0].shape[1:]), pieces[0].dtype),
+        out_shape=pltpu.VMEM((total, *pieces[0].shape[1:]), pieces[0].dtype),
         in_specs=[VMEM] * len(pieces),
         out_specs=VMEM,
+        compiler_params=pltpu.CompilerParams(vmem_limit_bytes=4 * 1024 * 1024),
     )(*in_vmem(pieces))
 
 
@@ -152,6 +153,7 @@
         out_shape=[half_shape] * 2 + [jax.ShapeDtypeStruct((bands,), jnp.float32)],
         in_specs=[SMEM] * 2 + [VMEM] * 2,
         out_specs=[VMEM] * 2 + [SMEM],
+        compiler_params=pltpu.CompilerParams(vmem_limit_bytes=4 * 1024 * 1024),
     )(counts, k_minus_q, occupation.T, screened)
 
     slabs = elements[0].reshape(n_z, bands, n_state, g_slab)
@@ -204,9 +206,15 @@
         compiler_params=limit,
     )(weights, *in_vmem([a_sorted, product, ring_k[4], ring_r[4]]))
 
-    share = jnp.sum(lax.all_to_all(shares, "ga", 0, 0, tiled=True), axis=0)
-    copies = jnp.broadcast_to(share[None], (lax.axis_size("pb"), *share.shape))
-    return jnp.sum(lax.all_to_all(copies, "pb", 0, 0, tiled=True), axis=0)
+    layers = [[2 * z_at + x_at for x_at in range(2)] for z_at in range(n_z)]
+    by_z = [[2 * z_at + x_at for z_at in range(n_z)] for x_at in range(2)]
+    shares = shares.reshape(n_z, 2, *shares.shape[1:])
+    share = jnp.sum(lax.all_to_all(shares, "ga", 0, 0, axis_index_groups=by_z, tiled=True), axis=0)
+    n_pb = lax.axis_size("pb")
+    copies = jnp.broadcast_to(share[None], (n_pb, *share.shape)).reshape(n_pb * 2, *share.shape[1:])
+    planes = [[p * groups + i for p in range(n_pb) for i in layer] for layer in layers]
+    received = lax.all_to_all(copies, ("pb", "ga"), 0, 0, axis_index_groups=planes, tiled=True)
+    return jnp.sum(received, axis=0)
 
 
 def solution(mesh):

time: 133 us -> 131 us (0.985)
  starting transfers between devices: 45.3 us -> 48.1 us
  blocking collectives: 33.6 us -> 31 us
  Pallas kernels: 11.5 us -> 9.04 us
  local copies, waits for them, and re-layouts: 4.08 us -> 2.68 us
    ppermute x24, starting transfers between devices: 42.4 us -> 46 us  [over_z(): lax.ppermute(value, 'ga', [(i, (i + 2 * k) % groups) for i in range(group...]
    all_to_all x2, blocking collectives: 33.6 us -> 31 us  [the longest x1 18.4 us: on_device(): lax.all_to_all(copies, ('pb', 'ga'), 0, 0, axis_index_groups=planes, tile...]
    unnamed x6 -> x4, local copies, waits for them, and re-layouts: 1.51 us -> 0.01 us
  transfers between devices with their start and end apart: 26 -> 26, of which waited for: 16 -> 10; matrix products, arithmetic and copies ran while one was open for 1% -> 1% of each run, Pallas kernels for 5% -> 5%
where the time goes in v4:
time: 131 us; the launch traced here: 130 us
  starting transfers between devices  48.1 us (37%)
  waiting for transfers between devices  37.4 us (29%)
  blocking collectives  31 us (24%)
  Pallas kernels  9.04 us (7%)
  local copies, waits for them, and re-layouts  2.68 us (2%)
  between operations  1.43 us (1%)
    ppermute x24, starting transfers between devices, over_z(): lax.ppermute(value, 'ga', [(i, (i + 2 * k) % groups) for i in range(group...  46 us
    ppermute x24, waiting for transfers between devices, over_z(): lax.ppermute(value, 'ga', [(i, (i + 2 * k) % groups) for i in range(group...  37.4 us
    all_to_all x1, blocking collectives, on_device(): lax.all_to_all(copies, ('pb', 'ga'), 0, 0, axis_index_groups=planes, tile...  18.4 us
    all_to_all x1, blocking collectives, on_device(): lax.all_to_all(shares, 'ga', 0, 0, axis_index_groups=by_z, tiled=True)  12.6 us
    pallas_call x1, Pallas kernels, on_device(): pl.pallas_call(functools.partial(contract_most, n_z), out_shape=[jax.Shap...  5.04 us
    pallas_call x1, Pallas kernels, on_device(): pl.pallas_call(functools.partial(contract_rest, n_z), out_shape=jax.Shape...  2.94 us
  transfers between devices with their start and end apart: 26, of which 10 were waited for; matrix products, arithmetic and copies ran while one was open for 1% of the time, Pallas kernels for 5%

profile of v4, /device:TPU:1, one launch (start us, length us, event | category | flops | bytes accessed | tf_op | source)
XLA Modules:
  0.0 130.3 jit_solution(7832853058364846033)
XLA Ops:
  1.7 2.5 %collective-permute-start = (bf16[8,112,128]{2,1,0:T(8,128)(2,1)S(1)}, bf16[8,112,128]{2,1,0:T(8,128)(2,1)S(1)}, u32[]{:S(2)}, u32[]{:S(2)}) collective-permute-start(bf16[8,112,128]{2,1,0:T(8,128)(2,1)S(1)} %get-tuple-element.68), channel_id=1, source_target_pairs={{0,2},{1,3},{2,4},{3,5},{4,6},{5,7},{6,8},{7,9},{8,10},{9,11},{10,... | collective-permute-start | bytes 688136 | tf_op jit(solution)/shard_map/ppermute | solution.py:149
  4.2 4.0 %collective-permute-start.1 = (bf16[8,112,128]{2,1,0:T(8,128)(2,1)S(1)}, bf16[8,112,128]{2,1,0:T(8,128)(2,1)S(1)}, u32[]{:S(2)}, u32[]{:S(2)}) collective-permute-start(bf16[8,112,128]{2,1,0:T(8,128)(2,1)S(1)} %get-tuple-element.67), channel_id=1, source_target_pairs={{0,14},{1,15},{2,0},{3,1},{4,2},{5,3},{6,4},{7,5},{8,6},{9,7},{10,... | collective-permute-start | bytes 688136 | tf_op jit(solution)/shard_map/ppermute | solution.py:149
  9.3 3.6 %collective-permute-start.8 = (bf16[4,112,128]{2,1,0:T(8,128)(2,1)S(1)}, bf16[4,112,128]{2,1,0:T(8,128)(2,1)S(1)}, u32[]{:S(2)}, u32[]{:S(2)}) collective-permute-start(bf16[4,112,128]{2,1,0:T(8,128)(2,1)S(1)} %get-tuple-element.61), channel_id=1, source_target_pairs={{0,12},{1,13},{2,14},{3,15},{4,0},{5,1},{6,2},{7,3},{8,4},{9,5},{1... | collective-permute-start | bytes 344072 | tf_op jit(solution)/shard_map/ppermute | solution.py:149
  13.5 4.3 %collective-permute-done.6 = bf16[4,112,128]{2,1,0:T(8,128)(2,1)S(1)} collective-permute-done((bf16[4,112,128]{2,1,0:T(8,128)(2,1)S(1)}, bf16[4,112,128]{2,1,0:T(8,128)(2,1)S(1)}, u32[]{:S(2)}, u32[]{:S(2)}) %collective-permute-start.6) | collective-permute-done | bytes 114720 | tf_op jit(solution)/shard_map/ppermute | solution.py:149
  23.7 2.8 %collective-permute-start.5 = (bf16[8,112,128]{2,1,0:T(8,128)(2,1)S(1)}, bf16[8,112,128]{2,1,0:T(8,128)(2,1)S(1)}, u32[]{:S(2)}, u32[]{:S(2)}) collective-permute-start(bf16[8,112,128]{2,1,0:T(8,128)(2,1)S(1)} %get-tuple-element.63), channel_id=1, source_target_pairs={{0,10},{1,11},{2,12},{3,13},{4,14},{5,15},{6,0},{7,1},{8,2},{9,3},... | collective-permute-start | bytes 688136 | tf_op jit(solution)/shard_map/ppermute | solution.py:149
  26.5 4.0 %collective-permute-start.7 = (bf16[4,112,128]{2,1,0:T(8,128)(2,1)S(1)}, bf16[4,112,128]{2,1,0:T(8,128)(2,1)S(1)}, u32[]{:S(2)}, u32[]{:S(2)}) collective-permute-start(bf16[4,112,128]{2,1,0:T(8,128)(2,1)S(1)} %collective-permute-done.6), channel_id=1, source_target_pairs={{0,4},{1,5},{2,6},{3,7},{4,8},{5,9},{6,10},{7,11},{8,12},{9,13},{1... | collective-permute-start | bytes 344072 | tf_op jit(solution)/shard_map/ppermute | solution.py:149
  30.8 13.2 %collective-permute-done.4.refs_3_ = bf16[8,112,128]{2,1,0:T(8,128)(2,1)S(1)} collective-permute-done((bf16[8,112,128]{2,1,0:T(8,128)(2,1)S(1)}, bf16[8,112,128]{2,1,0:T(8,128)(2,1)S(1)}, u32[]{:S(2)}, u32[]{:S(2)}) %collective-permute-start.4) | collective-permute-done | bytes 229408 | tf_op jit(solution)/shard_map/ppermute | solution.py:149
  44.0 2.4 %collective-permute-done.7.refs_4_ = bf16[4,112,128]{2,1,0:T(8,128)(2,1)S(1)} collective-permute-done((bf16[4,112,128]{2,1,0:T(8,128)(2,1)S(1)}, bf16[4,112,128]{2,1,0:T(8,128)(2,1)S(1)}, u32[]{:S(2)}, u32[]{:S(2)}) %collective-permute-start.7) | collective-permute-done | bytes 114720 | tf_op jit(solution)/shard_map/ppermute | solution.py:149
  47.4 2.1 %collective-permute-start.18 = (bf16[128,1024]{1,0:T(8,128)(2,1)S(1)}, bf16[128,1024]{1,0:T(8,128)(2,1)S(1)}, u32[]{:S(2)}, u32[]{:S(2)}) collective-permute-start(bf16[128,1024]{1,0:T(8,128)(2,1)S(1)} %get-tuple-element.50.refs_2_), channel_id=1, source_target_pairs={{0,2},{1,3},{2,4},{3,5},{4,6},{5,7},{6,8},{7,9},{8,10},{9,11},{10,... | collective-permute-start | bytes 786440 | tf_op jit(solution)/shard_map/ppermute | solution.py:149
  49.5 3.5 %collective-permute-start.19 = (bf16[128,1024]{1,0:T(8,128)(2,1)S(1)}, bf16[128,1024]{1,0:T(8,128)(2,1)S(1)}, u32[]{:S(2)}, u32[]{:S(2)}) collective-permute-start(bf16[128,1024]{1,0:T(8,128)(2,1)S(1)} %get-tuple-element.50.refs_2_), channel_id=1, source_target_pairs={{0,14},{1,15},{2,0},{3,1},{4,2},{5,3},{6,4},{7,5},{8,6},{9,7},{10,... | collective-permute-start | bytes 786440 | tf_op jit(solution)/shard_map/ppermute | solution.py:149
  53.0 2.7 %collective-permute-start.12 = (bf16[128,1024]{1,0:T(8,128)(2,1)S(1)}, bf16[128,1024]{1,0:T(8,128)(2,1)S(1)}, u32[]{:S(2)}, u32[]{:S(2)}) collective-permute-start(bf16[128,1024]{1,0:T(8,128)(2,1)S(1)} %collective-permute-done.10.refs_9_), channel_id=1, source_target_pairs={{0,14},{1,15},{2,0},{3,1},{4,2},{5,3},{6,4},{7,5},{8,6},{9,7},{10,... | collective-permute-start | bytes 786440 | tf_op jit(solution)/shard_map/ppermute | solution.py:149
  57.4 2.4 %collective-permute-start.21 = (bf16[128,1024]{1,0:T(8,128)(2,1)S(1)}, bf16[128,1024]{1,0:T(8,128)(2,1)S(1)}, u32[]{:S(2)}, u32[]{:S(2)}) collective-permute-start(bf16[128,1024]{1,0:T(8,128)(2,1)S(1)} %collective-permute-done.19.refs_8_), channel_id=1, source_target_pairs={{0,14},{1,15},{2,0},{3,1},{4,2},{5,3},{6,4},{7,5},{8,6},{9,7},{10,... | collective-permute-start | bytes 786440 | tf_op jit(solution)/shard_map/ppermute | solution.py:149
  59.8 2.9 %collective-permute-done.11.refs_10_ = bf16[128,1024]{1,0:T(8,128)(2,1)S(1)} collective-permute-done((bf16[128,1024]{1,0:T(8,128)(2,1)S(1)}, bf16[128,1024]{1,0:T(8,128)(2,1)S(1)}, u32[]{:S(2)}, u32[]{:S(2)}) %collective-permute-start.11) | collective-permute-done | bytes 262176 | tf_op jit(solution)/shard_map/ppermute | solution.py:149
  62.7 2.7 %collective-permute-start.14 = (bf16[128,1024]{1,0:T(8,128)(2,1)S(1)}, bf16[128,1024]{1,0:T(8,128)(2,1)S(1)}, u32[]{:S(2)}, u32[]{:S(2)}) collective-permute-start(bf16[128,1024]{1,0:T(8,128)(2,1)S(1)} %collective-permute-done.12.refs_15_), channel_id=1, source_target_pairs={{0,14},{1,15},{2,0},{3,1},{4,2},{5,3},{6,4},{7,5},{8,6},{9,7},{10,... | collective-permute-start | bytes 786440 | tf_op jit(solution)/shard_map/ppermute | solution.py:149
  65.4 2.9 %collective-permute-done.20.refs_4_ = bf16[128,1024]{1,0:T(8,128)(2,1)S(1)} collective-permute-done((bf16[128,1024]{1,0:T(8,128)(2,1)S(1)}, bf16[128,1024]{1,0:T(8,128)(2,1)S(1)}, u32[]{:S(2)}, u32[]{:S(2)}) %collective-permute-start.20) | collective-permute-done | bytes 262176 | tf_op jit(solution)/shard_map/ppermute | solution.py:149
  68.6 2.4 %collective-permute-start.23 = (bf16[128,1024]{1,0:T(8,128)(2,1)S(1)}, bf16[128,1024]{1,0:T(8,128)(2,1)S(1)}, u32[]{:S(2)}, u32[]{:S(2)}) collective-permute-start(bf16[128,1024]{1,0:T(8,128)(2,1)S(1)} %collective-permute-done.21.refs_7_), channel_id=1, source_target_pairs={{0,14},{1,15},{2,0},{3,1},{4,2},{5,3},{6,4},{7,5},{8,6},{9,7},{10,... | collective-permute-start | bytes 786440 | tf_op jit(solution)/shard_map/ppermute | solution.py:149
  71.0 2.9 %collective-permute-done.13.refs_11_ = bf16[128,1024]{1,0:T(8,128)(2,1)S(1)} collective-permute-done((bf16[128,1024]{1,0:T(8,128)(2,1)S(1)}, bf16[128,1024]{1,0:T(8,128)(2,1)S(1)}, u32[]{:S(2)}, u32[]{:S(2)}) %collective-permute-start.13) | collective-permute-done | bytes 262176 | tf_op jit(solution)/shard_map/ppermute | solution.py:149
  76.6 2.9 %collective-permute-done.22.refs_5_ = bf16[128,1024]{1,0:T(8,128)(2,1)S(1)} collective-permute-done((bf16[128,1024]{1,0:T(8,128)(2,1)S(1)}, bf16[128,1024]{1,0:T(8,128)(2,1)S(1)}, u32[]{:S(2)}, u32[]{:S(2)}) %collective-permute-start.22) | collective-permute-done | bytes 262176 | tf_op jit(solution)/shard_map/ppermute | solution.py:149
  81.0 4.1 %collective-permute-done.15.refs_12_ = bf16[128,1024]{1,0:T(8,128)(2,1)S(1)} collective-permute-done((bf16[128,1024]{1,0:T(8,128)(2,1)S(1)}, bf16[128,1024]{1,0:T(8,128)(2,1)S(1)}, u32[]{:S(2)}, u32[]{:S(2)}) %collective-permute-start.15) | collective-permute-done | bytes 262176 | tf_op jit(solution)/shard_map/ppermute | solution.py:149
  85.2 5.4 %collective-permute-start.25 = (bf16[128,1024]{1,0:T(8,128)(2,1)S(1)}, bf16[128,1024]{1,0:T(8,128)(2,1)S(1)}, u32[]{:S(2)}, u32[]{:S(2)}) collective-permute-start(bf16[128,1024]{1,0:T(8,128)(2,1)S(1)} %collective-permute-done.16.refs_13_), channel_id=1, source_target_pairs={{0,14},{1,15},{2,0},{3,1},{4,2},{5,3},{6,4},{7,5},{8,6},{9,7},{10,... | collective-permute-start | bytes 786440 | tf_op jit(solution)/shard_map/ppermute | solution.py:149
  90.5 5.0 %shard_map.57 = (bf16[16,8,112,128]{3,2,1,0:T(8,128)(2,1)S(1)}, f32[4,224,1024]{2,1,0:T(8,128)S(1)}) custom-call(bf16[64,112,128]{2,1,0:T(8,128)(2,1)S(1)} %shard_map.56.refs_0_, bf16[64,112,128]{2,1,0:T(8,128)(2,1)S(1)} %collective-permute-done.17.refs_1_, bf16[128,1024]{1,0:T(8,128)(2,1)S(1)} %get-tuple-element.50.refs_2_, ...), custom_call_target="tpu_custom_call" | custom-call | tf_op jit(solution)/shard_map/pallas_call | solution.py:189
  95.6 2.9 %shard_map.58 = f32[16,7,112]{2,1,0:T(8,128)S(1)} custom-call(f32[8]{0:T(128)S(1)} %get-tuple-element.33.weights, bf16[16,8,112,128]{3,2,1,0:T(8,128)(2,1)S(1)} %get-tuple-element.59.a_sorted, f32[4,224,1024]{2,1,0:T(8,128)S(1)} %get-tuple-element.60.product, bf16[128,1024]{1,0:T(8,128)(2,1)S(1)} %collective-permute-done.24.far_keep, ...), custom_call_target="tpu_custom_call" | custom-call | tf_op jit(solution)/shard_map/pallas_call | solution.py:200
  98.6 12.6 %all_to_all.10 = f32[8,2,7,112]{3,1,2,0:T(2,128)S(1)} all-to-all(f32[8,2,7,112]{3,1,2,0:T(2,128)S(1)} %copy.10), channel_id=1, replica_groups={{0,2,4,6,8,10,12,14},{1,3,5,7,9,11,13,15},{16,18,20,22,24,26,28,30},{17..., dimensions={0} | all-to-all | bytes 100352 | tf_op jit(solution)/shard_map/all_to_all | solution.py:212
  111.2 18.4 %all_to_all.11 = f32[32,7,112]{2,1,0:T(8,128)S(1)} all-to-all(f32[32,7,112]{2,1,0:T(8,128)S(1)} %bitcast.26), channel_id=1, replica_groups={{0,1,16,17,32,33,48,49,64,65,80,81,96,97,112,113,128,129,144,145,160,16..., dimensions={0} | all-to-all | bytes 200704 | tf_op jit(solution)/shard_map/all_to_all | solution.py:216
  (45 shorter events, 16.3 us)
Async XLA Ops:
  1.7 20.4 %collective-permute-start = (bf16[8,112,128]{2,1,0:T(8,128)(2,1)S(1)}, bf16[8,112,128]{2,1,0:T(8,128)(2,1)S(1)}, u32[]{:S(2)}, u32[]{:S(2)}) collective-permute-start(bf16[8,112,128]{2,1,0:T(8,128)(2,1)S(1)} %get-tuple-element.68), channel_id=1, source_target_pairs={{0,2},{1,3},{2,4},{3,5},{4,6},{5,7},{6,8},{7,9},{8,10},{9,11},{10,... | collective-permute-start | bytes 688136 | tf_op jit(solution)/shard_map/ppermute | solution.py:149
  4.2 19.5 %collective-permute-start.1 = (bf16[8,112,128]{2,1,0:T(8,128)(2,1)S(1)}, bf16[8,112,128]{2,1,0:T(8,128)(2,1)S(1)}, u32[]{:S(2)}, u32[]{:S(2)}) collective-permute-start(bf16[8,112,128]{2,1,0:T(8,128)(2,1)S(1)} %get-tuple-element.67), channel_id=1, source_target_pairs={{0,14},{1,15},{2,0},{3,1},{4,2},{5,3},{6,4},{7,5},{8,6},{9,7},{10,... | collective-permute-start | bytes 688136 | tf_op jit(solution)/shard_map/ppermute | solution.py:149
  9.3 11.4 %collective-permute-start.8 = (bf16[4,112,128]{2,1,0:T(8,128)(2,1)S(1)}, bf16[4,112,128]{2,1,0:T(8,128)(2,1)S(1)}, u32[]{:S(2)}, u32[]{:S(2)}) collective-permute-start(bf16[4,112,128]{2,1,0:T(8,128)(2,1)S(1)} %get-tuple-element.61), channel_id=1, source_target_pairs={{0,12},{1,13},{2,14},{3,15},{4,0},{5,1},{6,2},{7,3},{8,4},{9,5},{1... | collective-permute-start | bytes 344072 | tf_op jit(solution)/shard_map/ppermute | solution.py:149
  12.9 13.7 %collective-permute-start.2 = (bf16[8,112,128]{2,1,0:T(8,128)(2,1)S(1)}, bf16[8,112,128]{2,1,0:T(8,128)(2,1)S(1)}, u32[]{:S(2)}, u32[]{:S(2)}) collective-permute-start(bf16[8,112,128]{2,1,0:T(8,128)(2,1)S(1)} %get-tuple-element.66), channel_id=1, source_target_pairs={{0,4},{1,5},{2,6},{3,7},{4,8},{5,9},{6,10},{7,11},{8,12},{9,13},{1... | collective-permute-start | bytes 688136 | tf_op jit(solution)/shard_map/ppermute | solution.py:149
  17.8 12.7 %collective-permute-start.3 = (bf16[8,112,128]{2,1,0:T(8,128)(2,1)S(1)}, bf16[8,112,128]{2,1,0:T(8,128)(2,1)S(1)}, u32[]{:S(2)}, u32[]{:S(2)}) collective-permute-start(bf16[8,112,128]{2,1,0:T(8,128)(2,1)S(1)} %get-tuple-element.65), channel_id=1, source_target_pairs={{0,12},{1,13},{2,14},{3,15},{4,0},{5,1},{6,2},{7,3},{8,4},{9,5},{1... | collective-permute-start | bytes 688136 | tf_op jit(solution)/shard_map/ppermute | solution.py:149
  20.7 25.8 %collective-permute-start.10 = (bf16[128,1024]{1,0:T(8,128)(2,1)S(1)}, bf16[128,1024]{1,0:T(8,128)(2,1)S(1)}, u32[]{:S(2)}, u32[]{:S(2)}) collective-permute-start(bf16[128,1024]{1,0:T(8,128)(2,1)S(1)} %get-tuple-element.35), channel_id=1, source_target_pairs={{0,1},{1,0},{2,3},{3,2},{4,5},{5,4},{6,7},{7,6},{8,9},{9,8},{10,11... | collective-permute-start | bytes 786440 | tf_op jit(solution)/shard_map/ppermute | solution.py:146
  22.0 21.9 %collective-permute-start.4 = (bf16[8,112,128]{2,1,0:T(8,128)(2,1)S(1)}, bf16[8,112,128]{2,1,0:T(8,128)(2,1)S(1)}, u32[]{:S(2)}, u32[]{:S(2)}) collective-permute-start(bf16[8,112,128]{2,1,0:T(8,128)(2,1)S(1)} %get-tuple-element.64), channel_id=1, source_target_pairs={{0,6},{1,7},{2,8},{3,9},{4,10},{5,11},{6,12},{7,13},{8,14},{9,15},... | collective-permute-start | bytes 688136 | tf_op jit(solution)/shard_map/ppermute | solution.py:149
  23.7 20.2 %collective-permute-start.5 = (bf16[8,112,128]{2,1,0:T(8,128)(2,1)S(1)}, bf16[8,112,128]{2,1,0:T(8,128)(2,1)S(1)}, u32[]{:S(2)}, u32[]{:S(2)}) collective-permute-start(bf16[8,112,128]{2,1,0:T(8,128)(2,1)S(1)} %get-tuple-element.63), channel_id=1, source_target_pairs={{0,10},{1,11},{2,12},{3,13},{4,14},{5,15},{6,0},{7,1},{8,2},{9,3},... | collective-permute-start | bytes 688136 | tf_op jit(solution)/shard_map/ppermute | solution.py:149
  26.5 19.9 %collective-permute-start.7 = (bf16[4,112,128]{2,1,0:T(8,128)(2,1)S(1)}, bf16[4,112,128]{2,1,0:T(8,128)(2,1)S(1)}, u32[]{:S(2)}, u32[]{:S(2)}) collective-permute-start(bf16[4,112,128]{2,1,0:T(8,128)(2,1)S(1)} %collective-permute-done.6), channel_id=1, source_target_pairs={{0,4},{1,5},{2,6},{3,7},{4,8},{5,9},{6,10},{7,11},{8,12},{9,13},{1... | collective-permute-start | bytes 344072 | tf_op jit(solution)/shard_map/ppermute | solution.py:149
  30.5 16.1 %collective-permute-start.9 = (bf16[4,112,128]{2,1,0:T(8,128)(2,1)S(1)}, bf16[4,112,128]{2,1,0:T(8,128)(2,1)S(1)}, u32[]{:S(2)}, u32[]{:S(2)}) collective-permute-start(bf16[4,112,128]{2,1,0:T(8,128)(2,1)S(1)} %collective-permute-done.8), channel_id=1, source_target_pairs={{0,12},{1,13},{2,14},{3,15},{4,0},{5,1},{6,2},{7,3},{8,4},{9,5},{1... | collective-permute-start | bytes 344072 | tf_op jit(solution)/shard_map/ppermute | solution.py:149
  46.7 38.5 %collective-permute-start.17 = (bf16[64,112,128]{2,1,0:T(8,128)(2,1)S(1)}, bf16[64,112,128]{2,1,0:T(8,128)(2,1)S(1)}, u32[]{:S(2)}, u32[]{:S(2)}) collective-permute-start(bf16[64,112,128]{2,1,0:T(8,128)(2,1)S(1)} %shard_map.56.refs_0_), channel_id=1, source_target_pairs={{0,1},{1,0},{2,3},{3,2},{4,5},{5,4},{6,7},{7,6},{8,9},{9,8},{10,11... | collective-permute-start | bytes 5505032 | tf_op jit(solution)/shard_map/ppermute | solution.py:146
  47.4 9.6 %collective-permute-start.18 = (bf16[128,1024]{1,0:T(8,128)(2,1)S(1)}, bf16[128,1024]{1,0:T(8,128)(2,1)S(1)}, u32[]{:S(2)}, u32[]{:S(2)}) collective-permute-start(bf16[128,1024]{1,0:T(8,128)(2,1)S(1)} %get-tuple-element.50.refs_2_), channel_id=1, source_target_pairs={{0,2},{1,3},{2,4},{3,5},{4,6},{5,7},{6,8},{7,9},{8,10},{9,11},{10,... | collective-permute-start | bytes 786440 | tf_op jit(solution)/shard_map/ppermute | solution.py:149
  53.0 9.7 %collective-permute-start.11 = (bf16[128,1024]{1,0:T(8,128)(2,1)S(1)}, bf16[128,1024]{1,0:T(8,128)(2,1)S(1)}, u32[]{:S(2)}, u32[]{:S(2)}) collective-permute-start(bf16[128,1024]{1,0:T(8,128)(2,1)S(1)} %collective-permute-done.10.refs_9_), channel_id=1, source_target_pairs={{0,2},{1,3},{2,4},{3,5},{4,6},{5,7},{6,8},{7,9},{8,10},{9,11},{10,... | collective-permute-start | bytes 786440 | tf_op jit(solution)/shard_map/ppermute | solution.py:149
  53.0 9.7 %collective-permute-start.12 = (bf16[128,1024]{1,0:T(8,128)(2,1)S(1)}, bf16[128,1024]{1,0:T(8,128)(2,1)S(1)}, u32[]{:S(2)}, u32[]{:S(2)}) collective-permute-start(bf16[128,1024]{1,0:T(8,128)(2,1)S(1)} %collective-permute-done.10.refs_9_), channel_id=1, source_target_pairs={{0,14},{1,15},{2,0},{3,1},{4,2},{5,3},{6,4},{7,5},{8,6},{9,7},{10,... | collective-permute-start | bytes 786440 | tf_op jit(solution)/shard_map/ppermute | solution.py:149
  57.1 11.2 %collective-permute-start.20 = (bf16[128,1024]{1,0:T(8,128)(2,1)S(1)}, bf16[128,1024]{1,0:T(8,128)(2,1)S(1)}, u32[]{:S(2)}, u32[]{:S(2)}) collective-permute-start(bf16[128,1024]{1,0:T(8,128)(2,1)S(1)} %collective-permute-done.18.refs_3_), channel_id=1, source_target_pairs={{0,2},{1,3},{2,4},{3,5},{4,6},{5,7},{6,8},{7,9},{8,10},{9,11},{10,... | collective-permute-start | bytes 786440 | tf_op jit(solution)/shard_map/ppermute | solution.py:149
  57.4 10.9 %collective-permute-start.21 = (bf16[128,1024]{1,0:T(8,128)(2,1)S(1)}, bf16[128,1024]{1,0:T(8,128)(2,1)S(1)}, u32[]{:S(2)}, u32[]{:S(2)}) collective-permute-start(bf16[128,1024]{1,0:T(8,128)(2,1)S(1)} %collective-permute-done.19.refs_8_), channel_id=1, source_target_pairs={{0,14},{1,15},{2,0},{3,1},{4,2},{5,3},{6,4},{7,5},{8,6},{9,7},{10,... | collective-permute-start | bytes 786440 | tf_op jit(solution)/shard_map/ppermute | solution.py:149
  62.7 11.2 %collective-permute-start.13 = (bf16[128,1024]{1,0:T(8,128)(2,1)S(1)}, bf16[128,1024]{1,0:T(8,128)(2,1)S(1)}, u32[]{:S(2)}, u32[]{:S(2)}) collective-permute-start(bf16[128,1024]{1,0:T(8,128)(2,1)S(1)} %collective-permute-done.11.refs_10_), channel_id=1, source_target_pairs={{0,2},{1,3},{2,4},{3,5},{4,6},{5,7},{6,8},{7,9},{8,10},{9,11},{10,... | collective-permute-start | bytes 786440 | tf_op jit(solution)/shard_map/ppermute | solution.py:149
  62.7 11.2 %collective-permute-start.14 = (bf16[128,1024]{1,0:T(8,128)(2,1)S(1)}, bf16[128,1024]{1,0:T(8,128)(2,1)S(1)}, u32[]{:S(2)}, u32[]{:S(2)}) collective-permute-start(bf16[128,1024]{1,0:T(8,128)(2,1)S(1)} %collective-permute-done.12.refs_15_), channel_id=1, source_target_pairs={{0,14},{1,15},{2,0},{3,1},{4,2},{5,3},{6,4},{7,5},{8,6},{9,7},{10,... | collective-permute-start | bytes 786440 | tf_op jit(solution)/shard_map/ppermute | solution.py:149
  68.3 11.2 %collective-permute-start.22 = (bf16[128,1024]{1,0:T(8,128)(2,1)S(1)}, bf16[128,1024]{1,0:T(8,128)(2,1)S(1)}, u32[]{:S(2)}, u32[]{:S(2)}) collective-permute-start(bf16[128,1024]{1,0:T(8,128)(2,1)S(1)} %collective-permute-done.20.refs_4_), channel_id=1, source_target_pairs={{0,2},{1,3},{2,4},{3,5},{4,6},{5,7},{6,8},{7,9},{8,10},{9,11},{10,... | collective-permute-start | bytes 786440 | tf_op jit(solution)/shard_map/ppermute | solution.py:149
  68.6 10.9 %collective-permute-start.23 = (bf16[128,1024]{1,0:T(8,128)(2,1)S(1)}, bf16[128,1024]{1,0:T(8,128)(2,1)S(1)}, u32[]{:S(2)}, u32[]{:S(2)}) collective-permute-start(bf16[128,1024]{1,0:T(8,128)(2,1)S(1)} %collective-permute-done.21.refs_7_), channel_id=1, source_target_pairs={{0,14},{1,15},{2,0},{3,1},{4,2},{5,3},{6,4},{7,5},{8,6},{9,7},{10,... | collective-permute-start | bytes 786440 | tf_op jit(solution)/shard_map/ppermute | solution.py:149
  73.9 11.2 %collective-permute-start.15 = (bf16[128,1024]{1,0:T(8,128)(2,1)S(1)}, bf16[128,1024]{1,0:T(8,128)(2,1)S(1)}, u32[]{:S(2)}, u32[]{:S(2)}) collective-permute-start(bf16[128,1024]{1,0:T(8,128)(2,1)S(1)} %collective-permute-done.13.refs_11_), channel_id=1, source_target_pairs={{0,2},{1,3},{2,4},{3,5},{4,6},{5,7},{6,8},{7,9},{8,10},{9,11},{10,... | collective-permute-start | bytes 786440 | tf_op jit(solution)/shard_map/ppermute | solution.py:149
  75.4 9.8 %collective-permute-start.16 = (bf16[128,1024]{1,0:T(8,128)(2,1)S(1)}, bf16[128,1024]{1,0:T(8,128)(2,1)S(1)}, u32[]{:S(2)}, u32[]{:S(2)}) collective-permute-start(bf16[128,1024]{1,0:T(8,128)(2,1)S(1)} %collective-permute-done.14.refs_14_), channel_id=1, source_target_pairs={{0,14},{1,15},{2,0},{3,1},{4,2},{5,3},{6,4},{7,5},{8,6},{9,7},{10,... | collective-permute-start | bytes 786440 | tf_op jit(solution)/shard_map/ppermute | solution.py:149
  79.6 16.0 %collective-permute-start.24 = (bf16[128,1024]{1,0:T(8,128)(2,1)S(1)}, bf16[128,1024]{1,0:T(8,128)(2,1)S(1)}, u32[]{:S(2)}, u32[]{:S(2)}) collective-permute-start(bf16[128,1024]{1,0:T(8,128)(2,1)S(1)} %collective-permute-done.22.refs_5_), channel_id=1, source_target_pairs={{0,2},{1,3},{2,4},{3,5},{4,6},{5,7},{6,8},{7,9},{8,10},{9,11},{10,... | collective-permute-start | bytes 786440 | tf_op jit(solution)/shard_map/ppermute | solution.py:149
  85.2 10.4 %collective-permute-start.25 = (bf16[128,1024]{1,0:T(8,128)(2,1)S(1)}, bf16[128,1024]{1,0:T(8,128)(2,1)S(1)}, u32[]{:S(2)}, u32[]{:S(2)}) collective-permute-start(bf16[128,1024]{1,0:T(8,128)(2,1)S(1)} %collective-permute-done.16.refs_13_), channel_id=1, source_target_pairs={{0,14},{1,15},{2,0},{3,1},{4,2},{5,3},{6,4},{7,5},{8,6},{9,7},{10,... | collective-permute-start | bytes 786440 | tf_op jit(solution)/shard_map/ppermute | solution.py:149
  (4 other events, 55.6 us)

commit v5 on v4

--- a/solution.py
+++ b/solution.py
@@ -11,7 +11,7 @@
 LANES = 128
 VMEM = pl.BlockSpec(memory_space=pltpu.VMEM)
 SMEM = pl.BlockSpec(memory_space=pltpu.SMEM)
-STEP = 2
+STEP = 8
 
 
 def position():

time: 131 us -> 130 us (level)
  transfers between devices with their start and end apart: 26 -> 26, of which waited for: 10 -> 10; matrix products, arithmetic and copies ran while one was open for 1% -> 1% of each run, Pallas kernels for 5% -> 4%
where the time goes in v5:
time: 130 us
  starting transfers between devices  48.1 us (37%)
  waiting for transfers between devices  37.4 us (29%)
  blocking collectives  31.6 us (24%)
  Pallas kernels  7.78 us (6%)
  local copies, waits for them, and re-layouts  2.68 us (2%)
  between operations  1.43 us (1%)
    ppermute x24, starting transfers between devices, over_z(): lax.ppermute(value, 'ga', [(i, (i + 2 * k) % groups) for i in range(group...  46 us
    ppermute x24, waiting for transfers between devices, over_z(): lax.ppermute(value, 'ga', [(i, (i + 2 * k) % groups) for i in range(group...  37.4 us
    all_to_all x1, blocking collectives, on_device(): lax.all_to_all(copies, ('pb', 'ga'), 0, 0, axis_index_groups=planes, tile...  18.4 us
    all_to_all x1, blocking collectives, on_device(): lax.all_to_all(shares, 'ga', 0, 0, axis_index_groups=by_z, tiled=True)  13.2 us
    pallas_call x1, Pallas kernels, on_device(): pl.pallas_call(functools.partial(contract_most, n_z), out_shape=[jax.Shap...  4.44 us
  transfers between devices with their start and end apart: 26, of which 10 were waited for; matrix products, arithmetic and copies ran while one was open for 1% of the time, Pallas kernels for 4%

profile of v5, /device:TPU:1, one launch (start us, length us, event | category | flops | bytes accessed | tf_op | source)
XLA Modules:
  0.0 129.6 jit_solution(8640287020689096829)
XLA Ops:
  1.7 2.5 %collective-permute-start = (bf16[8,112,128]{2,1,0:T(8,128)(2,1)S(1)}, bf16[8,112,128]{2,1,0:T(8,128)(2,1)S(1)}, u32[]{:S(2)}, u32[]{:S(2)}) collective-permute-start(bf16[8,112,128]{2,1,0:T(8,128)(2,1)S(1)} %get-tuple-element.68), channel_id=1, source_target_pairs={{0,2},{1,3},{2,4},{3,5},{4,6},{5,7},{6,8},{7,9},{8,10},{9,11},{10,... | collective-permute-start | bytes 688136 | tf_op jit(solution)/shard_map/ppermute | solution.py:149
  4.2 4.0 %collective-permute-start.1 = (bf16[8,112,128]{2,1,0:T(8,128)(2,1)S(1)}, bf16[8,112,128]{2,1,0:T(8,128)(2,1)S(1)}, u32[]{:S(2)}, u32[]{:S(2)}) collective-permute-start(bf16[8,112,128]{2,1,0:T(8,128)(2,1)S(1)} %get-tuple-element.67), channel_id=1, source_target_pairs={{0,14},{1,15},{2,0},{3,1},{4,2},{5,3},{6,4},{7,5},{8,6},{9,7},{10,... | collective-permute-start | bytes 688136 | tf_op jit(solution)/shard_map/ppermute | solution.py:149
  9.3 3.6 %collective-permute-start.8 = (bf16[4,112,128]{2,1,0:T(8,128)(2,1)S(1)}, bf16[4,112,128]{2,1,0:T(8,128)(2,1)S(1)}, u32[]{:S(2)}, u32[]{:S(2)}) collective-permute-start(bf16[4,112,128]{2,1,0:T(8,128)(2,1)S(1)} %get-tuple-element.61), channel_id=1, source_target_pairs={{0,12},{1,13},{2,14},{3,15},{4,0},{5,1},{6,2},{7,3},{8,4},{9,5},{1... | collective-permute-start | bytes 344072 | tf_op jit(solution)/shard_map/ppermute | solution.py:149
  13.5 4.3 %collective-permute-done.6 = bf16[4,112,128]{2,1,0:T(8,128)(2,1)S(1)} collective-permute-done((bf16[4,112,128]{2,1,0:T(8,128)(2,1)S(1)}, bf16[4,112,128]{2,1,0:T(8,128)(2,1)S(1)}, u32[]{:S(2)}, u32[]{:S(2)}) %collective-permute-start.6) | collective-permute-done | bytes 114720 | tf_op jit(solution)/shard_map/ppermute | solution.py:149
  23.7 2.8 %collective-permute-start.5 = (bf16[8,112,128]{2,1,0:T(8,128)(2,1)S(1)}, bf16[8,112,128]{2,1,0:T(8,128)(2,1)S(1)}, u32[]{:S(2)}, u32[]{:S(2)}) collective-permute-start(bf16[8,112,128]{2,1,0:T(8,128)(2,1)S(1)} %get-tuple-element.63), channel_id=1, source_target_pairs={{0,10},{1,11},{2,12},{3,13},{4,14},{5,15},{6,0},{7,1},{8,2},{9,3},... | collective-permute-start | bytes 688136 | tf_op jit(solution)/shard_map/ppermute | solution.py:149
  26.5 4.0 %collective-permute-start.7 = (bf16[4,112,128]{2,1,0:T(8,128)(2,1)S(1)}, bf16[4,112,128]{2,1,0:T(8,128)(2,1)S(1)}, u32[]{:S(2)}, u32[]{:S(2)}) collective-permute-start(bf16[4,112,128]{2,1,0:T(8,128)(2,1)S(1)} %collective-permute-done.6), channel_id=1, source_target_pairs={{0,4},{1,5},{2,6},{3,7},{4,8},{5,9},{6,10},{7,11},{8,12},{9,13},{1... | collective-permute-start | bytes 344072 | tf_op jit(solution)/shard_map/ppermute | solution.py:149
  30.8 13.2 %collective-permute-done.4.refs_3_ = bf16[8,112,128]{2,1,0:T(8,128)(2,1)S(1)} collective-permute-done((bf16[8,112,128]{2,1,0:T(8,128)(2,1)S(1)}, bf16[8,112,128]{2,1,0:T(8,128)(2,1)S(1)}, u32[]{:S(2)}, u32[]{:S(2)}) %collective-permute-start.4) | collective-permute-done | bytes 229408 | tf_op jit(solution)/shard_map/ppermute | solution.py:149
  44.0 2.4 %collective-permute-done.7.refs_4_ = bf16[4,112,128]{2,1,0:T(8,128)(2,1)S(1)} collective-permute-done((bf16[4,112,128]{2,1,0:T(8,128)(2,1)S(1)}, bf16[4,112,128]{2,1,0:T(8,128)(2,1)S(1)}, u32[]{:S(2)}, u32[]{:S(2)}) %collective-permute-start.7) | collective-permute-done | bytes 114720 | tf_op jit(solution)/shard_map/ppermute | solution.py:149
  47.4 2.1 %collective-permute-start.18 = (bf16[128,1024]{1,0:T(8,128)(2,1)S(1)}, bf16[128,1024]{1,0:T(8,128)(2,1)S(1)}, u32[]{:S(2)}, u32[]{:S(2)}) collective-permute-start(bf16[128,1024]{1,0:T(8,128)(2,1)S(1)} %get-tuple-element.50.refs_2_), channel_id=1, source_target_pairs={{0,2},{1,3},{2,4},{3,5},{4,6},{5,7},{6,8},{7,9},{8,10},{9,11},{10,... | collective-permute-start | bytes 786440 | tf_op jit(solution)/shard_map/ppermute | solution.py:149
  49.5 3.5 %collective-permute-start.19 = (bf16[128,1024]{1,0:T(8,128)(2,1)S(1)}, bf16[128,1024]{1,0:T(8,128)(2,1)S(1)}, u32[]{:S(2)}, u32[]{:S(2)}) collective-permute-start(bf16[128,1024]{1,0:T(8,128)(2,1)S(1)} %get-tuple-element.50.refs_2_), channel_id=1, source_target_pairs={{0,14},{1,15},{2,0},{3,1},{4,2},{5,3},{6,4},{7,5},{8,6},{9,7},{10,... | collective-permute-start | bytes 786440 | tf_op jit(solution)/shard_map/ppermute | solution.py:149
  53.0 2.7 %collective-permute-start.12 = (bf16[128,1024]{1,0:T(8,128)(2,1)S(1)}, bf16[128,1024]{1,0:T(8,128)(2,1)S(1)}, u32[]{:S(2)}, u32[]{:S(2)}) collective-permute-start(bf16[128,1024]{1,0:T(8,128)(2,1)S(1)} %collective-permute-done.10.refs_9_), channel_id=1, source_target_pairs={{0,14},{1,15},{2,0},{3,1},{4,2},{5,3},{6,4},{7,5},{8,6},{9,7},{10,... | collective-permute-start | bytes 786440 | tf_op jit(solution)/shard_map/ppermute | solution.py:149
  57.4 2.4 %collective-permute-start.21 = (bf16[128,1024]{1,0:T(8,128)(2,1)S(1)}, bf16[128,1024]{1,0:T(8,128)(2,1)S(1)}, u32[]{:S(2)}, u32[]{:S(2)}) collective-permute-start(bf16[128,1024]{1,0:T(8,128)(2,1)S(1)} %collective-permute-done.19.refs_8_), channel_id=1, source_target_pairs={{0,14},{1,15},{2,0},{3,1},{4,2},{5,3},{6,4},{7,5},{8,6},{9,7},{10,... | collective-permute-start | bytes 786440 | tf_op jit(solution)/shard_map/ppermute | solution.py:149
  59.8 2.9 %collective-permute-done.11.refs_10_ = bf16[128,1024]{1,0:T(8,128)(2,1)S(1)} collective-permute-done((bf16[128,1024]{1,0:T(8,128)(2,1)S(1)}, bf16[128,1024]{1,0:T(8,128)(2,1)S(1)}, u32[]{:S(2)}, u32[]{:S(2)}) %collective-permute-start.11) | collective-permute-done | bytes 262176 | tf_op jit(solution)/shard_map/ppermute | solution.py:149
  62.7 2.7 %collective-permute-start.14 = (bf16[128,1024]{1,0:T(8,128)(2,1)S(1)}, bf16[128,1024]{1,0:T(8,128)(2,1)S(1)}, u32[]{:S(2)}, u32[]{:S(2)}) collective-permute-start(bf16[128,1024]{1,0:T(8,128)(2,1)S(1)} %collective-permute-done.12.refs_15_), channel_id=1, source_target_pairs={{0,14},{1,15},{2,0},{3,1},{4,2},{5,3},{6,4},{7,5},{8,6},{9,7},{10,... | collective-permute-start | bytes 786440 | tf_op jit(solution)/shard_map/ppermute | solution.py:149
  65.4 2.9 %collective-permute-done.20.refs_4_ = bf16[128,1024]{1,0:T(8,128)(2,1)S(1)} collective-permute-done((bf16[128,1024]{1,0:T(8,128)(2,1)S(1)}, bf16[128,1024]{1,0:T(8,128)(2,1)S(1)}, u32[]{:S(2)}, u32[]{:S(2)}) %collective-permute-start.20) | collective-permute-done | bytes 262176 | tf_op jit(solution)/shard_map/ppermute | solution.py:149
  68.6 2.4 %collective-permute-start.23 = (bf16[128,1024]{1,0:T(8,128)(2,1)S(1)}, bf16[128,1024]{1,0:T(8,128)(2,1)S(1)}, u32[]{:S(2)}, u32[]{:S(2)}) collective-permute-start(bf16[128,1024]{1,0:T(8,128)(2,1)S(1)} %collective-permute-done.21.refs_7_), channel_id=1, source_target_pairs={{0,14},{1,15},{2,0},{3,1},{4,2},{5,3},{6,4},{7,5},{8,6},{9,7},{10,... | collective-permute-start | bytes 786440 | tf_op jit(solution)/shard_map/ppermute | solution.py:149
  71.0 2.9 %collective-permute-done.13.refs_11_ = bf16[128,1024]{1,0:T(8,128)(2,1)S(1)} collective-permute-done((bf16[128,1024]{1,0:T(8,128)(2,1)S(1)}, bf16[128,1024]{1,0:T(8,128)(2,1)S(1)}, u32[]{:S(2)}, u32[]{:S(2)}) %collective-permute-start.13) | collective-permute-done | bytes 262176 | tf_op jit(solution)/shard_map/ppermute | solution.py:149
  76.6 2.9 %collective-permute-done.22.refs_5_ = bf16[128,1024]{1,0:T(8,128)(2,1)S(1)} collective-permute-done((bf16[128,1024]{1,0:T(8,128)(2,1)S(1)}, bf16[128,1024]{1,0:T(8,128)(2,1)S(1)}, u32[]{:S(2)}, u32[]{:S(2)}) %collective-permute-start.22) | collective-permute-done | bytes 262176 | tf_op jit(solution)/shard_map/ppermute | solution.py:149
  81.0 4.1 %collective-permute-done.15.refs_12_ = bf16[128,1024]{1,0:T(8,128)(2,1)S(1)} collective-permute-done((bf16[128,1024]{1,0:T(8,128)(2,1)S(1)}, bf16[128,1024]{1,0:T(8,128)(2,1)S(1)}, u32[]{:S(2)}, u32[]{:S(2)}) %collective-permute-start.15) | collective-permute-done | bytes 262176 | tf_op jit(solution)/shard_map/ppermute | solution.py:149
  85.2 5.4 %collective-permute-start.25 = (bf16[128,1024]{1,0:T(8,128)(2,1)S(1)}, bf16[128,1024]{1,0:T(8,128)(2,1)S(1)}, u32[]{:S(2)}, u32[]{:S(2)}) collective-permute-start(bf16[128,1024]{1,0:T(8,128)(2,1)S(1)} %collective-permute-done.16.refs_13_), channel_id=1, source_target_pairs={{0,14},{1,15},{2,0},{3,1},{4,2},{5,3},{6,4},{7,5},{8,6},{9,7},{10,... | collective-permute-start | bytes 786440 | tf_op jit(solution)/shard_map/ppermute | solution.py:149
  90.5 4.4 %shard_map.57 = (bf16[16,8,112,128]{3,2,1,0:T(8,128)(2,1)S(1)}, f32[1,896,1024]{2,1,0:T(8,128)S(1)}) custom-call(bf16[64,112,128]{2,1,0:T(8,128)(2,1)S(1)} %shard_map.56.refs_0_, bf16[64,112,128]{2,1,0:T(8,128)(2,1)S(1)} %collective-permute-done.17.refs_1_, bf16[128,1024]{1,0:T(8,128)(2,1)S(1)} %get-tuple-element.50.refs_2_, ...), custom_call_target="tpu_custom_call" | custom-call | tf_op jit(solution)/shard_map/pallas_call | solution.py:189
  95.0 2.3 %shard_map.58 = f32[16,7,112]{2,1,0:T(8,128)S(1)} custom-call(f32[8]{0:T(128)S(1)} %get-tuple-element.33.weights, bf16[16,8,112,128]{3,2,1,0:T(8,128)(2,1)S(1)} %get-tuple-element.59.a_sorted, f32[1,896,1024]{2,1,0:T(8,128)S(1)} %get-tuple-element.60.product, bf16[128,1024]{1,0:T(8,128)(2,1)S(1)} %collective-permute-done.24.far_keep, ...), custom_call_target="tpu_custom_call" | custom-call | tf_op jit(solution)/shard_map/pallas_call | solution.py:200
  97.3 13.2 %all_to_all.10 = f32[8,2,7,112]{3,1,2,0:T(2,128)S(1)} all-to-all(f32[8,2,7,112]{3,1,2,0:T(2,128)S(1)} %copy.10), channel_id=1, replica_groups={{0,2,4,6,8,10,12,14},{1,3,5,7,9,11,13,15},{16,18,20,22,24,26,28,30},{17..., dimensions={0} | all-to-all | bytes 100352 | tf_op jit(solution)/shard_map/all_to_all | solution.py:212
  110.6 18.4 %all_to_all.11 = f32[32,7,112]{2,1,0:T(8,128)S(1)} all-to-all(f32[32,7,112]{2,1,0:T(8,128)S(1)} %bitcast.26), channel_id=1, replica_groups={{0,1,16,17,32,33,48,49,64,65,80,81,96,97,112,113,128,129,144,145,160,16..., dimensions={0} | all-to-all | bytes 200704 | tf_op jit(solution)/shard_map/all_to_all | solution.py:216
  (45 shorter events, 16.3 us)
Async XLA Ops:
  1.7 20.4 %collective-permute-start = (bf16[8,112,128]{2,1,0:T(8,128)(2,1)S(1)}, bf16[8,112,128]{2,1,0:T(8,128)(2,1)S(1)}, u32[]{:S(2)}, u32[]{:S(2)}) collective-permute-start(bf16[8,112,128]{2,1,0:T(8,128)(2,1)S(1)} %get-tuple-element.68), channel_id=1, source_target_pairs={{0,2},{1,3},{2,4},{3,5},{4,6},{5,7},{6,8},{7,9},{8,10},{9,11},{10,... | collective-permute-start | bytes 688136 | tf_op jit(solution)/shard_map/ppermute | solution.py:149
  4.2 19.5 %collective-permute-start.1 = (bf16[8,112,128]{2,1,0:T(8,128)(2,1)S(1)}, bf16[8,112,128]{2,1,0:T(8,128)(2,1)S(1)}, u32[]{:S(2)}, u32[]{:S(2)}) collective-permute-start(bf16[8,112,128]{2,1,0:T(8,128)(2,1)S(1)} %get-tuple-element.67), channel_id=1, source_target_pairs={{0,14},{1,15},{2,0},{3,1},{4,2},{5,3},{6,4},{7,5},{8,6},{9,7},{10,... | collective-permute-start | bytes 688136 | tf_op jit(solution)/shard_map/ppermute | solution.py:149
  9.3 11.4 %collective-permute-start.8 = (bf16[4,112,128]{2,1,0:T(8,128)(2,1)S(1)}, bf16[4,112,128]{2,1,0:T(8,128)(2,1)S(1)}, u32[]{:S(2)}, u32[]{:S(2)}) collective-permute-start(bf16[4,112,128]{2,1,0:T(8,128)(2,1)S(1)} %get-tuple-element.61), channel_id=1, source_target_pairs={{0,12},{1,13},{2,14},{3,15},{4,0},{5,1},{6,2},{7,3},{8,4},{9,5},{1... | collective-permute-start | bytes 344072 | tf_op jit(solution)/shard_map/ppermute | solution.py:149
  12.9 13.7 %collective-permute-start.2 = (bf16[8,112,128]{2,1,0:T(8,128)(2,1)S(1)}, bf16[8,112,128]{2,1,0:T(8,128)(2,1)S(1)}, u32[]{:S(2)}, u32[]{:S(2)}) collective-permute-start(bf16[8,112,128]{2,1,0:T(8,128)(2,1)S(1)} %get-tuple-element.66), channel_id=1, source_target_pairs={{0,4},{1,5},{2,6},{3,7},{4,8},{5,9},{6,10},{7,11},{8,12},{9,13},{1... | collective-permute-start | bytes 688136 | tf_op jit(solution)/shard_map/ppermute | solution.py:149
  17.8 12.7 %collective-permute-start.3 = (bf16[8,112,128]{2,1,0:T(8,128)(2,1)S(1)}, bf16[8,112,128]{2,1,0:T(8,128)(2,1)S(1)}, u32[]{:S(2)}, u32[]{:S(2)}) collective-permute-start(bf16[8,112,128]{2,1,0:T(8,128)(2,1)S(1)} %get-tuple-element.65), channel_id=1, source_target_pairs={{0,12},{1,13},{2,14},{3,15},{4,0},{5,1},{6,2},{7,3},{8,4},{9,5},{1... | collective-permute-start | bytes 688136 | tf_op jit(solution)/shard_map/ppermute | solution.py:149
  20.7 25.8 %collective-permute-start.10 = (bf16[128,1024]{1,0:T(8,128)(2,1)S(1)}, bf16[128,1024]{1,0:T(8,128)(2,1)S(1)}, u32[]{:S(2)}, u32[]{:S(2)}) collective-permute-start(bf16[128,1024]{1,0:T(8,128)(2,1)S(1)} %get-tuple-element.35), channel_id=1, source_target_pairs={{0,1},{1,0},{2,3},{3,2},{4,5},{5,4},{6,7},{7,6},{8,9},{9,8},{10,11... | collective-permute-start | bytes 786440 | tf_op jit(solution)/shard_map/ppermute | solution.py:146
  22.0 21.9 %collective-permute-start.4 = (bf16[8,112,128]{2,1,0:T(8,128)(2,1)S(1)}, bf16[8,112,128]{2,1,0:T(8,128)(2,1)S(1)}, u32[]{:S(2)}, u32[]{:S(2)}) collective-permute-start(bf16[8,112,128]{2,1,0:T(8,128)(2,1)S(1)} %get-tuple-element.64), channel_id=1, source_target_pairs={{0,6},{1,7},{2,8},{3,9},{4,10},{5,11},{6,12},{7,13},{8,14},{9,15},... | collective-permute-start | bytes 688136 | tf_op jit(solution)/shard_map/ppermute | solution.py:149
  23.7 20.2 %collective-permute-start.5 = (bf16[8,112,128]{2,1,0:T(8,128)(2,1)S(1)}, bf16[8,112,128]{2,1,0:T(8,128)(2,1)S(1)}, u32[]{:S(2)}, u32[]{:S(2)}) collective-permute-start(bf16[8,112,128]{2,1,0:T(8,128)(2,1)S(1)} %get-tuple-element.63), channel_id=1, source_target_pairs={{0,10},{1,11},{2,12},{3,13},{4,14},{5,15},{6,0},{7,1},{8,2},{9,3},... | collective-permute-start | bytes 688136 | tf_op jit(solution)/shard_map/ppermute | solution.py:149
  26.5 19.9 %collective-permute-start.7 = (bf16[4,112,128]{2,1,0:T(8,128)(2,1)S(1)}, bf16[4,112,128]{2,1,0:T(8,128)(2,1)S(1)}, u32[]{:S(2)}, u32[]{:S(2)}) collective-permute-start(bf16[4,112,128]{2,1,0:T(8,128)(2,1)S(1)} %collective-permute-done.6), channel_id=1, source_target_pairs={{0,4},{1,5},{2,6},{3,7},{4,8},{5,9},{6,10},{7,11},{8,12},{9,13},{1... | collective-permute-start | bytes 344072 | tf_op jit(solution)/shard_map/ppermute | solution.py:149
  30.5 16.1 %collective-permute-start.9 = (bf16[4,112,128]{2,1,0:T(8,128)(2,1)S(1)}, bf16[4,112,128]{2,1,0:T(8,128)(2,1)S(1)}, u32[]{:S(2)}, u32[]{:S(2)}) collective-permute-start(bf16[4,112,128]{2,1,0:T(8,128)(2,1)S(1)} %collective-permute-done.8), channel_id=1, source_target_pairs={{0,12},{1,13},{2,14},{3,15},{4,0},{5,1},{6,2},{7,3},{8,4},{9,5},{1... | collective-permute-start | bytes 344072 | tf_op jit(solution)/shard_map/ppermute | solution.py:149
  46.7 38.5 %collective-permute-start.17 = (bf16[64,112,128]{2,1,0:T(8,128)(2,1)S(1)}, bf16[64,112,128]{2,1,0:T(8,128)(2,1)S(1)}, u32[]{:S(2)}, u32[]{:S(2)}) collective-permute-start(bf16[64,112,128]{2,1,0:T(8,128)(2,1)S(1)} %shard_map.56.refs_0_), channel_id=1, source_target_pairs={{0,1},{1,0},{2,3},{3,2},{4,5},{5,4},{6,7},{7,6},{8,9},{9,8},{10,11... | collective-permute-start | bytes 5505032 | tf_op jit(solution)/shard_map/ppermute | solution.py:146
  47.4 9.6 %collective-permute-start.18 = (bf16[128,1024]{1,0:T(8,128)(2,1)S(1)}, bf16[128,1024]{1,0:T(8,128)(2,1)S(1)}, u32[]{:S(2)}, u32[]{:S(2)}) collective-permute-start(bf16[128,1024]{1,0:T(8,128)(2,1)S(1)} %get-tuple-element.50.refs_2_), channel_id=1, source_target_pairs={{0,2},{1,3},{2,4},{3,5},{4,6},{5,7},{6,8},{7,9},{8,10},{9,11},{10,... | collective-permute-start | bytes 786440 | tf_op jit(solution)/shard_map/ppermute | solution.py:149
  53.0 9.7 %collective-permute-start.11 = (bf16[128,1024]{1,0:T(8,128)(2,1)S(1)}, bf16[128,1024]{1,0:T(8,128)(2,1)S(1)}, u32[]{:S(2)}, u32[]{:S(2)}) collective-permute-start(bf16[128,1024]{1,0:T(8,128)(2,1)S(1)} %collective-permute-done.10.refs_9_), channel_id=1, source_target_pairs={{0,2},{1,3},{2,4},{3,5},{4,6},{5,7},{6,8},{7,9},{8,10},{9,11},{10,... | collective-permute-start | bytes 786440 | tf_op jit(solution)/shard_map/ppermute | solution.py:149
  53.0 9.7 %collective-permute-start.12 = (bf16[128,1024]{1,0:T(8,128)(2,1)S(1)}, bf16[128,1024]{1,0:T(8,128)(2,1)S(1)}, u32[]{:S(2)}, u32[]{:S(2)}) collective-permute-start(bf16[128,1024]{1,0:T(8,128)(2,1)S(1)} %collective-permute-done.10.refs_9_), channel_id=1, source_target_pairs={{0,14},{1,15},{2,0},{3,1},{4,2},{5,3},{6,4},{7,5},{8,6},{9,7},{10,... | collective-permute-start | bytes 786440 | tf_op jit(solution)/shard_map/ppermute | solution.py:149
  57.1 11.2 %collective-permute-start.20 = (bf16[128,1024]{1,0:T(8,128)(2,1)S(1)}, bf16[128,1024]{1,0:T(8,128)(2,1)S(1)}, u32[]{:S(2)}, u32[]{:S(2)}) collective-permute-start(bf16[128,1024]{1,0:T(8,128)(2,1)S(1)} %collective-permute-done.18.refs_3_), channel_id=1, source_target_pairs={{0,2},{1,3},{2,4},{3,5},{4,6},{5,7},{6,8},{7,9},{8,10},{9,11},{10,... | collective-permute-start | bytes 786440 | tf_op jit(solution)/shard_map/ppermute | solution.py:149
  57.4 10.9 %collective-permute-start.21 = (bf16[128,1024]{1,0:T(8,128)(2,1)S(1)}, bf16[128,1024]{1,0:T(8,128)(2,1)S(1)}, u32[]{:S(2)}, u32[]{:S(2)}) collective-permute-start(bf16[128,1024]{1,0:T(8,128)(2,1)S(1)} %collective-permute-done.19.refs_8_), channel_id=1, source_target_pairs={{0,14},{1,15},{2,0},{3,1},{4,2},{5,3},{6,4},{7,5},{8,6},{9,7},{10,... | collective-permute-start | bytes 786440 | tf_op jit(solution)/shard_map/ppermute | solution.py:149
  62.7 11.2 %collective-permute-start.13 = (bf16[128,1024]{1,0:T(8,128)(2,1)S(1)}, bf16[128,1024]{1,0:T(8,128)(2,1)S(1)}, u32[]{:S(2)}, u32[]{:S(2)}) collective-permute-start(bf16[128,1024]{1,0:T(8,128)(2,1)S(1)} %collective-permute-done.11.refs_10_), channel_id=1, source_target_pairs={{0,2},{1,3},{2,4},{3,5},{4,6},{5,7},{6,8},{7,9},{8,10},{9,11},{10,... | collective-permute-start | bytes 786440 | tf_op jit(solution)/shard_map/ppermute | solution.py:149
  62.7 11.2 %collective-permute-start.14 = (bf16[128,1024]{1,0:T(8,128)(2,1)S(1)}, bf16[128,1024]{1,0:T(8,128)(2,1)S(1)}, u32[]{:S(2)}, u32[]{:S(2)}) collective-permute-start(bf16[128,1024]{1,0:T(8,128)(2,1)S(1)} %collective-permute-done.12.refs_15_), channel_id=1, source_target_pairs={{0,14},{1,15},{2,0},{3,1},{4,2},{5,3},{6,4},{7,5},{8,6},{9,7},{10,... | collective-permute-start | bytes 786440 | tf_op jit(solution)/shard_map/ppermute | solution.py:149
  68.3 11.2 %collective-permute-start.22 = (bf16[128,1024]{1,0:T(8,128)(2,1)S(1)}, bf16[128,1024]{1,0:T(8,128)(2,1)S(1)}, u32[]{:S(2)}, u32[]{:S(2)}) collective-permute-start(bf16[128,1024]{1,0:T(8,128)(2,1)S(1)} %collective-permute-done.20.refs_4_), channel_id=1, source_target_pairs={{0,2},{1,3},{2,4},{3,5},{4,6},{5,7},{6,8},{7,9},{8,10},{9,11},{10,... | collective-permute-start | bytes 786440 | tf_op jit(solution)/shard_map/ppermute | solution.py:149
  68.6 10.9 %collective-permute-start.23 = (bf16[128,1024]{1,0:T(8,128)(2,1)S(1)}, bf16[128,1024]{1,0:T(8,128)(2,1)S(1)}, u32[]{:S(2)}, u32[]{:S(2)}) collective-permute-start(bf16[128,1024]{1,0:T(8,128)(2,1)S(1)} %collective-permute-done.21.refs_7_), channel_id=1, source_target_pairs={{0,14},{1,15},{2,0},{3,1},{4,2},{5,3},{6,4},{7,5},{8,6},{9,7},{10,... | collective-permute-start | bytes 786440 | tf_op jit(solution)/shard_map/ppermute | solution.py:149
  73.9 11.2 %collective-permute-start.15 = (bf16[128,1024]{1,0:T(8,128)(2,1)S(1)}, bf16[128,1024]{1,0:T(8,128)(2,1)S(1)}, u32[]{:S(2)}, u32[]{:S(2)}) collective-permute-start(bf16[128,1024]{1,0:T(8,128)(2,1)S(1)} %collective-permute-done.13.refs_11_), channel_id=1, source_target_pairs={{0,2},{1,3},{2,4},{3,5},{4,6},{5,7},{6,8},{7,9},{8,10},{9,11},{10,... | collective-permute-start | bytes 786440 | tf_op jit(solution)/shard_map/ppermute | solution.py:149
  75.4 9.8 %collective-permute-start.16 = (bf16[128,1024]{1,0:T(8,128)(2,1)S(1)}, bf16[128,1024]{1,0:T(8,128)(2,1)S(1)}, u32[]{:S(2)}, u32[]{:S(2)}) collective-permute-start(bf16[128,1024]{1,0:T(8,128)(2,1)S(1)} %collective-permute-done.14.refs_14_), channel_id=1, source_target_pairs={{0,14},{1,15},{2,0},{3,1},{4,2},{5,3},{6,4},{7,5},{8,6},{9,7},{10,... | collective-permute-start | bytes 786440 | tf_op jit(solution)/shard_map/ppermute | solution.py:149
  79.6 15.4 %collective-permute-start.24 = (bf16[128,1024]{1,0:T(8,128)(2,1)S(1)}, bf16[128,1024]{1,0:T(8,128)(2,1)S(1)}, u32[]{:S(2)}, u32[]{:S(2)}) collective-permute-start(bf16[128,1024]{1,0:T(8,128)(2,1)S(1)} %collective-permute-done.22.refs_5_), channel_id=1, source_target_pairs={{0,2},{1,3},{2,4},{3,5},{4,6},{5,7},{6,8},{7,9},{8,10},{9,11},{10,... | collective-permute-start | bytes 786440 | tf_op jit(solution)/shard_map/ppermute | solution.py:149
  85.2 9.8 %collective-permute-start.25 = (bf16[128,1024]{1,0:T(8,128)(2,1)S(1)}, bf16[128,1024]{1,0:T(8,128)(2,1)S(1)}, u32[]{:S(2)}, u32[]{:S(2)}) collective-permute-start(bf16[128,1024]{1,0:T(8,128)(2,1)S(1)} %collective-permute-done.16.refs_13_), channel_id=1, source_target_pairs={{0,14},{1,15},{2,0},{3,1},{4,2},{5,3},{6,4},{7,5},{8,6},{9,7},{10,... | collective-permute-start | bytes 786440 | tf_op jit(solution)/shard_map/ppermute | solution.py:149
  (4 other events, 55.6 us)
